TPU v7x, 256 devices: a whole 4x4x8 slice. The times are simulated.
256 devices in a mesh: segment: 4 (over x), expert: 32 (over z, y), dp: 2 (over core).
Axes of the slice: x: 4, y: 4, z: 8, core: 2. Of those that a mesh axis runs over, the one named last changes fastest.
Arguments:
- entering: bfloat16 [4, 4096, 2560], P('segment', ('expert', 'dp')), may hold values from -0.59765625 to 0.59765625
- fresh: bfloat16 [1, 4096, 2560], P(None, ('expert', 'dp')), may hold values from -0.59765625 to 0.59765625
- w_gate: bfloat16 [4, 64, 2560, 768], P('segment', ('expert', 'dp')), may hold values from -0.125 to 0.125
- w_up: bfloat16 [4, 64, 2560, 768], P('segment', ('expert', 'dp')), may hold values from -0.125 to 0.125
- w_down: bfloat16 [4, 64, 768, 2560], P('segment', ('expert', 'dp')), may hold values from -0.21875 to 0.21875
- router: bfloat16 [4, 2560, 64], P('segment'), may hold values from -0.0625 to 0.0625
- gain: float32 [4, 2560], P('segment'), may hold values from 0.5 to 2
- routes: int32 [4, 2, 4096, 6], P('segment', None, ('expert', 'dp')), may hold values from 0 to 63, all different within a row; in each aligned block of 64 rows (0 to 63, 64 to 127, ..., all dimensions but the last counted through in order) at most 8 rows name the same one
Outputs:
- section_out: bfloat16 [4, 2, 4096, 2560], P('segment', None, ('expert', 'dp'))
Inputs may be any that keep to these rules, and one draw needn't show every extreme that they name: `routes`: in every aligned block of 64 rows (the tokens of one device for one section and micro-batch) no expert is named by more than 8 rows, and in some blocks one expert is named by exactly 8 rows; a row names 6 different experts.
All inputs are finite; a program needn't handle non-finite values.
Results may differ from a plain program's by a relative error of at most 0.009.
Values may be sent and summed in bfloat16 or wider, within the bound.
No kernel may reach another device: no remote copies, remote signals or barrier semaphores. Data moves between devices by JAX's collectives and lax.ppermute only.
A program may use at most 64 MiB of HBM per device.

v0:
```python
import jax
import jax.numpy as jnp
from jax import lax
from jax.experimental import pallas as pl
from jax.experimental.pallas import tpu as pltpu
from jax.sharding import PartitionSpec as P

CAP = 8
LANES = 128
GROUP = ("expert", "dp")
Z, Y, C = 8, 4, 2
VMEM = pl.BlockSpec(memory_space=pltpu.VMEM)
BRIEF = pl.CostEstimate(flops=1000, transcendentals=0, bytes_accessed=1000)
SMEM = pl.BlockSpec(memory_space=pltpu.SMEM)


def dot(lhs, rhs, lhs_dim=1, rhs_dim=0):
    return lax.dot_general(
        lhs, rhs, (((lhs_dim,), (rhs_dim,)), ((), ())), preferred_element_type=jnp.float32
    )


def column_tiles(width, tile):
    return [slice(start, min(start + tile, width)) for start in range(0, width, tile)]


def iota(shape, dim):
    return lax.broadcasted_iota(jnp.int32, shape, dim)


def move(value, target):
    pairs = []
    for z in range(Z):
        for y in range(Y):
            for core in range(C):
                to_z, to_y, to_core = target(z, y, core)
                pairs.append(((z * Y + y) * C + core, ((to_z % Z) * Y + to_y % Y) * C + to_core))
    return lax.ppermute(value, GROUP, pairs)


def to_other_core(value):
    return move(value, lambda z, y, core: (z, y, 1 - core))


def along_y(value, steps):
    return value if steps == 0 else move(value, lambda z, y, core: (z, y + steps, core))


def along_z(value, steps):
    return move(value, lambda z, y, core: (z + steps, y, core))


def after(value, *others):
    return lax.optimization_barrier((value, *others))[0]


def prepare_kernel(step, first_ref, arrived_ref, fresh_ref, gain_ref, router_ref, picks_ref,
                   current_ref, packed_ref, weights_ref):
    tokens, width = current_ref.shape
    experts = router_ref.shape[0]
    current = jnp.where(first_ref[0] == 1, fresh_ref[...], arrived_ref[...])
    current_ref[...] = current
    values = current.astype(jnp.float32)
    inv_scale = lax.rsqrt(jnp.mean(values * values, axis=1, keepdims=True) + 1e-06)
    normed = (values * inv_scale * gain_ref[...]).astype(jnp.bfloat16)
    packed_ref[:, :width] = normed
    logits = dot(normed, router_ref[...], 1, 1)
    expert_ids = iota((experts, tokens), 0)
    chosen_rows = jnp.zeros((experts, tokens), jnp.float32)
    for choice in range(picks_ref.shape[0]):
        chosen_rows += jnp.where(picks_ref[choice, step : step + 1, :] == expert_ids, 1.0, 0.0)
    chosen_rows = chosen_rows.astype(jnp.bfloat16)
    row, column = iota((tokens, tokens), 0), iota((tokens, tokens), 1)
    chosen = dot(jnp.where(row == column, 1.0, 0.0).astype(jnp.bfloat16), chosen_rows, 1, 1)
    rank = dot(jnp.where(column < row, 1.0, 0.0).astype(jnp.bfloat16), chosen_rows, 1, 1)
    scores = chosen / (1.0 + jnp.exp(-logits))
    mixing = (scores / jnp.sum(scores, axis=1, keepdims=True)).astype(jnp.bfloat16)
    slot = jnp.where(chosen > 0.0, rank, float(CAP)).astype(jnp.bfloat16)
    packed_ref[:, width:] = jnp.concatenate([slot.astype(jnp.float32), mixing.astype(jnp.float32)], axis=1).astype(jnp.bfloat16)
    places = experts * CAP
    spread = jnp.where(iota((experts, places), 1) // CAP == iota((experts, places), 0), 1.0, 0.0).astype(jnp.bfloat16)
    here = dot(slot, spread) == (iota((tokens, places), 1) % CAP).astype(jnp.float32)
    weights_ref[...] = jnp.where(here, dot(mixing, spread), 0.0).astype(jnp.bfloat16)


def prepare(step, first, arrived, fresh, gain, router, picks):
    tokens, width = arrived.shape
    return pl.pallas_call(
        lambda *refs: prepare_kernel(step, *refs),
        out_shape=(
            jax.ShapeDtypeStruct((tokens, width), jnp.bfloat16),
            jax.ShapeDtypeStruct((tokens, width + LANES), jnp.bfloat16),
            jax.ShapeDtypeStruct((tokens, router.shape[0] * CAP), jnp.bfloat16),
        ),
        in_specs=[SMEM] + [VMEM] * 5,
        out_specs=(VMEM, VMEM, VMEM),
        cost_estimate=BRIEF,
        name="prepare",
    )(first, arrived, fresh, gain, router, picks)


def stacked(pieces):
    return jnp.concatenate([piece.astype(jnp.float32) for piece in pieces], axis=0).astype(jnp.bfloat16)


def dispatch_kernel(block, count, ids_ref, *refs):
    packed_refs, row_refs = refs[:count], refs[count:]
    width = row_refs[0].shape[1]
    rows = row_refs[0].shape[0]
    notes = jnp.concatenate([ref[:, width:] for ref in packed_refs], axis=0)
    tokens = notes.shape[0]
    line, lane = iota((2 * Y * C, LANES), 0), iota((2 * Y * C, LANES), 1)
    select = jnp.zeros((2 * Y * C, LANES), jnp.float32)
    for place in range(Y * C):
        hit = (line == place) & (lane == ids_ref[place])
        select = jnp.where(hit, 1.0, select)
    picked = dot(select.astype(jnp.bfloat16), notes, 1, 1)
    row, token = iota((rows, tokens), 0), iota((rows, tokens), 1)
    code = jnp.where(token // block == row // CAP, row % CAP, -1).astype(jnp.float32)
    picks = []
    for place in range(Y * C):
        here = jnp.broadcast_to(picked[place : place + 1, :], (rows, tokens)) == code
        picks.append(jnp.where(here, 1.0, 0.0))
    pick = jnp.concatenate(picks, axis=0).astype(jnp.bfloat16)

    for cols in column_tiles(width, 512):
        values = jnp.concatenate([ref[:, cols] for ref in packed_refs], axis=0)
        result = dot(pick, values)
        start = 0
        for ref in row_refs:
            ref[:, cols] = result[start : start + ref.shape[0]].astype(jnp.bfloat16)
            start += ref.shape[0]


def dispatch(ids, packed, block):
    width = packed[0].shape[1] - LANES
    tokens = sum(value.shape[0] for value in packed)
    rows = tokens // block * CAP
    return pl.pallas_call(
        lambda *refs: dispatch_kernel(block, len(packed), *refs),
        out_shape=[
            jax.ShapeDtypeStruct((count * rows, width), jnp.bfloat16) for count in (1, C - 1, *[C] * (Y - 1))
        ],
        in_specs=[SMEM] + [VMEM] * len(packed),
        out_specs=[VMEM] * (Y + 1),
        cost_estimate=BRIEF,
        name="dispatch",
    )(ids, *packed)


def travelled(sent):
    own, other = sent[:2]
    there = [along_y(value, step) for step, value in enumerate(sent[2:], 1)]
    return own, other, there


def exchanged(own, other, there):
    half = own.shape[0]
    return [own, *there, to_other_core(jnp.concatenate([other] + [value[half:] for value in there], axis=0))]


def experts_kernel(groups, places_ref, *refs):
    row_refs = [refs[index * (Y + 1) : (index + 1) * (Y + 1)] for index in range(groups)]
    gate_hbm, up_hbm, down_hbm, out_ref = refs[groups * (Y + 1) : groups * (Y + 1) + 4]
    gate_ref, up_ref, down_ref, gated_ref, upper_ref, hidden_ref, arrived = refs[groups * (Y + 1) + 4 :]
    width, inner = gate_ref.shape
    parts, tiles = column_tiles(width, 512), column_tiles(inner, 256)
    copies = []
    for index, part in enumerate(parts):
        for which, (source, target) in enumerate(((gate_hbm, gate_ref), (up_hbm, up_ref))):
            copies.append(pltpu.make_async_copy(source.at[part, :], target.at[part, :], arrived.at[2 * index + which]))
    last = pltpu.make_async_copy(down_hbm, down_ref, arrived.at[2 * len(parts)])
    for copy in copies:
        copy.start()
    last.start()
    gated_ref[...] = jnp.zeros(gated_ref.shape, jnp.float32)
    upper_ref[...] = jnp.zeros(upper_ref.shape, jnp.float32)

    def gather(index, carry):
        part = pl.ds(pl.multiple_of(index * 512, 512), 512)
        pieces = []
        for group in row_refs:
            half = group[0].shape[0]
            pieces += [ref[:half, part] for ref in group[:Y]] + [group[Y][:, part]]
        rows = stacked(pieces)
        for which, (source, target) in enumerate(((gate_hbm, gate_ref), (up_hbm, up_ref))):
            pltpu.make_async_copy(source.at[part, :], target.at[part, :], arrived.at[2 * index + which]).wait()
        for cols in tiles:
            gated_ref[:, cols] += dot(rows, gate_ref[part, cols])
            upper_ref[:, cols] += dot(rows, up_ref[part, cols])
        return carry

    lax.fori_loop(0, len(parts), gather, 0)
    for cols in tiles:
        gate = gated_ref[:, cols]
        hidden_ref[:, cols] = (gate / (1.0 + jnp.exp(-gate)) * upper_ref[:, cols]).astype(jnp.bfloat16)
    last.wait()

    def give(index, carry):
        cols = pl.ds(pl.multiple_of(index * 512, 512), 512)
        result = dot(hidden_ref[...], down_ref[:, cols])
        for place in range(out_ref.shape[0]):
            piece = result[place * CAP : (place + 1) * CAP].astype(jnp.bfloat16)
            out_ref[pl.ds(places_ref[place], 1), :, cols] = piece[None]
        return carry

    lax.fori_loop(0, width // 512, give, 0)


def run_experts(groups, places, w_gate, w_up, w_down):
    width, hidden = w_gate.shape
    operands = []
    for arrays in groups:
        operands += exchanged(*arrays)
    count = places.shape[0] * CAP
    return pl.pallas_call(
        lambda *refs: experts_kernel(len(groups), *refs),
        out_shape=jax.ShapeDtypeStruct((places.shape[0], CAP, width), jnp.bfloat16),
        in_specs=[SMEM] + [VMEM] * len(operands) + [pl.BlockSpec(memory_space=pl.ANY)] * 3,
        out_specs=VMEM,
        scratch_shapes=[
            pltpu.VMEM((width, hidden), jnp.bfloat16),
            pltpu.VMEM((width, hidden), jnp.bfloat16),
            pltpu.VMEM((hidden, width), jnp.bfloat16),
            pltpu.VMEM((count, hidden), jnp.float32),
            pltpu.VMEM((count, hidden), jnp.float32),
            pltpu.VMEM((count, hidden), jnp.bfloat16),
            pltpu.SemaphoreType.DMA((2 * len(column_tiles(width, 512)) + 1,)),
        ],
        compiler_params=pltpu.CompilerParams(vmem_limit_bytes=44 << 20),
        cost_estimate=BRIEF,
        name="experts",
    )(places, *operands, w_gate, w_up, w_down)


def combine_kernel(earlier, current_ref, weights_ref, landed_ref, *refs):
    out_ref = refs[-1]
    weights = weights_ref[...]
    for index in range(earlier):
        out_ref[index] = refs[index][0]
    for cols in column_tiles(out_ref.shape[2], 512):
        total = current_ref[:, cols].astype(jnp.float32) + dot(weights, landed_ref[:, cols])
        out_ref[earlier, :, cols] = total.astype(jnp.bfloat16)


def combine(current, weights, landed, *results):
    return pl.pallas_call(
        lambda *refs: combine_kernel(len(results), *refs),
        out_shape=jax.ShapeDtypeStruct((len(results) + 1, *current.shape), jnp.bfloat16),
        in_specs=[VMEM] * (3 + len(results)),
        out_specs=VMEM,
        cost_estimate=BRIEF,
        name="combine",
    )(current, weights, landed, *results)


NEAR, FAR = (0, -1, 1, -2, 2), (-3, 3, 4)


def section(packed, ids, places, w_gate, w_up, w_down):
    tokens = packed.shape[0]
    part = tokens // 2
    below, above = [packed], [packed]
    for _ in range(2):
        below.append(along_z(below[-1], 1))
        above.append(along_z(above[-1], -1))
    near_rows = dispatch(ids, [packed, below[1], above[1], below[2], above[2]], tokens)
    below.append(along_z(below[2], 1))
    above.append(along_z(above[2], -1))
    third = after(below[3], near_rows[0]), after(above[3], near_rows[0])
    far = [below[3], above[3], along_z(third[0][:part], 1), along_z(third[1][part:], -1)]
    far = far[:2] + [pltpu.with_memory_space_constraint(value, pltpu.VMEM) for value in far[2:]]
    far_rows = dispatch(ids, far, tokens)
    own, other, there = travelled(near_rows)
    near_there = own, other, [after(value, far_rows[0]) for value in there]
    outputs = run_experts([near_there, travelled(far_rows)], places, w_gate, w_up, w_down)
    landed = lax.all_to_all(outputs, GROUP, split_axis=0, concat_axis=0, tiled=True)
    return landed.reshape(-1, landed.shape[-1])


def shards(entering, fresh, w_gate, w_up, w_down, router, gain, routes):
    at_start = (lax.axis_index("segment") == 0).astype(jnp.int32).reshape(1)
    never = jnp.zeros((1,), jnp.int32)
    place, core = lax.axis_index("expert"), lax.axis_index("dp")
    z, y = place // Y, place % Y
    steps = jnp.arange(Y * C, dtype=jnp.int32)
    ids = (z * Y + (y + steps // C) % Y) * C + (core + steps % C) % C
    order = [(block, step, side) for group in (NEAR, FAR) for side in range(C) for step in range(Y) for block in group]
    block, step, side = (jnp.array(column, jnp.int32) for column in zip(*order))
    places = ((z + block + Z) % Z * Y + (y - step + Y) % Y) * C + (core + side) % C
    router_rows = jnp.transpose(router[0])
    picks = jnp.transpose(routes[0], (2, 0, 1))
    w_gate, w_up, w_down = (
        pltpu.with_memory_space_constraint(value[0, 0], pltpu.HBM) for value in (w_gate, w_up, w_down)
    )
    results = []
    count = lax.axis_size("segment")
    for index in range(routes.shape[1]):
        if index == 0:
            first, arrived, other = never, entering[0], entering[0]
        else:
            arrived = lax.ppermute(results[-1][0], "segment", [(i, i + 1) for i in range(count - 1)])
            first, other = at_start, fresh[index - 1]
        current, packed, weights = prepare(index, first, arrived, other, gain, router_rows, picks)
        landed = section(packed, ids, places, w_gate, w_up, w_down)
        results.append(combine(current, weights, landed, *(results if index == routes.shape[1] - 1 else [])))
    return results[-1][None]


def solution(mesh):
    tokens = P("segment", ("expert", "dp"), None)
    weights = P("segment", ("expert", "dp"), None, None)
    in_specs = (
        tokens, P(None, ("expert", "dp"), None), weights, weights, weights,
        P("segment", None, None), P("segment", None), P("segment", None, ("expert", "dp"), None),
    )
    out_specs = P("segment", None, ("expert", "dp"), None)
    return jax.shard_map(shards, mesh=mesh, in_specs=in_specs, out_specs=out_specs, check_vma=False)
```

profile of v0, /device:TPU:7, one launch (start us, length us, event | category | flops | bytes accessed | tf_op | source)
XLA Modules:
  0.0 309.0 jit_solution(11627777157985936344)
XLA Ops:
  0.0 2.7 prepare.2
  2.7 5.6 %collective-permute-start.1 = (bf16[64,2688]{1,0:T(8,128)(2,1)}, bf16[64,2688]{1,0:T(8,128)(2,1)S(1)}, u32[]{:S(2)}, u32[]{:S(2)}) collective-permute-start(bf16[64,2688]{1,0:T(8,128)(2,1)} %get-tuple-element.43.refs_1_), channel_id=1, source_target_pairs={{0,56},{1,57},{2,58},{3,59},{4,60},{5,61},{6,62},{7,63},{8,0},{9,1... | collective-permute-start | bytes 1032200 | tf_op jit(solution)/shard_map/ppermute | solution.py:38
  8.3 7.0 %collective-permute-done.1.refs_3_ = bf16[64,2688]{1,0:T(8,128)(2,1)S(1)} collective-permute-done((bf16[64,2688]{1,0:T(8,128)(2,1)}, bf16[64,2688]{1,0:T(8,128)(2,1)S(1)}, u32[]{:S(2)}, u32[]{:S(2)}) %collective-permute-start.1) | collective-permute-done | bytes 344096 | tf_op jit(solution)/shard_map/ppermute | solution.py:38
  15.3 3.3 %collective-permute-start.3 = (bf16[64,2688]{1,0:T(8,128)(2,1)S(1)}, bf16[64,2688]{1,0:T(8,128)(2,1)S(1)}, u32[]{:S(2)}, u32[]{:S(2)}) collective-permute-start(bf16[64,2688]{1,0:T(8,128)(2,1)S(1)} %collective-permute-done.1.refs_3_), channel_id=1, source_target_pairs={{0,56},{1,57},{2,58},{3,59},{4,60},{5,61},{6,62},{7,63},{8,0},{9,1... | collective-permute-start | bytes 1032200 | tf_op jit(solution)/shard_map/ppermute | solution.py:38
  18.6 5.8 %collective-permute-done.3.refs_5_ = bf16[64,2688]{1,0:T(8,128)(2,1)S(1)} collective-permute-done((bf16[64,2688]{1,0:T(8,128)(2,1)S(1)}, bf16[64,2688]{1,0:T(8,128)(2,1)S(1)}, u32[]{:S(2)}, u32[]{:S(2)}) %collective-permute-start.3) | collective-permute-done | bytes 344096 | tf_op jit(solution)/shard_map/ppermute | solution.py:38
  24.4 3.4 %collective-permute-start.6 = (bf16[64,2688]{1,0:T(8,128)(2,1)S(1)}, bf16[64,2688]{1,0:T(8,128)(2,1)S(1)}, u32[]{:S(2)}, u32[]{:S(2)}) collective-permute-start(bf16[64,2688]{1,0:T(8,128)(2,1)S(1)} %collective-permute-done.3.refs_5_), channel_id=1, source_target_pairs={{0,56},{1,57},{2,58},{3,59},{4,60},{5,61},{6,62},{7,63},{8,0},{9,1... | collective-permute-start | bytes 1032200 | tf_op jit(solution)/shard_map/ppermute | solution.py:38
  28.6 3.6 %dispatch.4 = (bf16[40,2560]{1,0:T(8,128)(2,1)}, bf16[40,2560]{1,0:T(8,128)(2,1)}, bf16[80,2560]{1,0:T(8,128)(2,1)}, bf16[80,2560]{1,0:T(8,128)(2,1)}, bf16[80,2560]{1,0:T(8,128)(2,1)}) custom-call(s32[8]{0:T(128)} %fusion.3.refs_0_, bf16[64,2688]{1,0:T(8,128)(2,1)} %get-tuple-element.43.refs_1_, bf16[64,2688]{1,0:T(8,128)(2,1)} %copy-done.11, ...), custom_call_target="tpu_custom_call" | custom-call | flops 1000 | bytes 1000 | tf_op jit(solution)/shard_map/dispatch/pallas_call | solution.py:139
  33.5 2.6 collective-permute-start.9
  37.2 2.6 collective-permute-start.8
  42.2 3.5 %collective-permute-done.7.refs_3_ = bf16[32,2688]{1,0:T(8,128)(2,1)S(1)} collective-permute-done((bf16[32,2688]{1,0:T(8,128)(2,1)S(1)}, bf16[32,2688]{1,0:T(8,128)(2,1)S(1)}, u32[]{:S(2)}, u32[]{:S(2)}) %collective-permute-start.7) | collective-permute-done | bytes 172064 | tf_op jit(solution)/shard_map/ppermute | solution.py:38
  45.7 2.6 dispatch.5
  54.6 4.6 %collective-permute-start.11 = (bf16[160,2560]{1,0:T(8,128)(2,1)S(1)}, bf16[160,2560]{1,0:T(8,128)(2,1)S(1)}, u32[]{:S(2)}, u32[]{:S(2)}) collective-permute-start(bf16[160,2560]{1,0:T(8,128)(2,1)S(1)} %pad_maximum_fusion), channel_id=1, source_target_pairs={{0,1},{1,0},{2,3},{3,2},{4,5},{5,4},{6,7},{7,6},{8,9},{9,8},{10,11... | collective-permute-start | bytes 2457608 | tf_op jit(solution)/shard_map/ppermute | solution.py:38
  59.2 2.9 collective-permute-done.13.refs_8_
  62.8 3.8 %collective-permute-start.15 = (bf16[96,2560]{1,0:T(8,128)(2,1)S(1)}, bf16[96,2560]{1,0:T(8,128)(2,1)S(1)}, u32[]{:S(2)}, u32[]{:S(2)}) collective-permute-start(bf16[96,2560]{1,0:T(8,128)(2,1)S(1)} %pad_maximum_fusion.2), channel_id=1, source_target_pairs={{0,1},{1,0},{2,3},{3,2},{4,5},{5,4},{6,7},{7,6},{8,9},{9,8},{10,11... | collective-permute-start | bytes 1474568 | tf_op jit(solution)/shard_map/ppermute | solution.py:38
  68.1 10.4 %experts.2 = bf16[64,8,2560]{2,1,0:T(8,128)(2,1)S(1)} custom-call(s32[64]{0:T(128)S(1)} %fusion.1.refs_0_, bf16[40,2560]{1,0:T(8,128)(2,1)S(1)} %copy-done, bf16[80,2560]{1,0:T(8,128)(2,1)S(1)} %collective-permute-done.4.refs_2_, bf16[80,2560]{1,0:T(8,128)(2,1)S(1)} %collective-permute-done.9.refs_3_, bf16[80,2560]{1,0:T(8,128)(2,1)S(1)} %collective-permute-done.10.refs_4_, ...), custom_call_target="tpu_custom_call" | custom-call | flops 1000 | bytes 1000 | tf_op jit(solution)/shard_map/experts/pallas_call | solution.py:216
  78.4 69.4 %all_to_all.10 = bf16[64,8,2560]{2,1,0:T(8,128)(2,1)} all-to-all(bf16[64,8,2560]{2,1,0:T(8,128)(2,1)S(1)} %experts.2), channel_id=1, replica_groups=mesh['segment'=4,'expert'=32,'dp'=2] {'expert','dp'}, dimensions={0} | all-to-all | bytes 5242880 | tf_op jit(solution)/shard_map/all_to_all | solution.py:277
  147.8 3.2 %combine.2.refs_3_ = bf16[1,64,2560]{2,1,0:T(8,128)(2,1)} custom-call(bf16[64,2560]{1,0:T(8,128)(2,1)} %get-tuple-element.41.refs_0_, bf16[64,512]{1,0:T(8,128)(2,1)} %get-tuple-element.42.refs_1_, bf16[512,2560]{1,0:T(8,128)(2,1)} %bitcast.23), custom_call_target="tpu_custom_call" | custom-call | flops 1000 | bytes 1000 | tf_op jit(solution)/shard_map/combine/pallas_call | solution.py:247
  152.3 9.7 %collective-permute-done.16.refs_1_ = bf16[64,2560]{1,0:T(8,128)(2,1)S(1)} collective-permute-done((bf16[64,2560]{1,0:T(8,128)(2,1)}, bf16[64,2560]{1,0:T(8,128)(2,1)S(1)}, u32[]{:S(2)}, u32[]{:S(2)}) %collective-permute-start.16) | collective-permute-done | bytes 327712 | tf_op jit(solution)/shard_map/ppermute | solution.py:302
  167.5 7.0 %collective-permute-done.18.refs_3_ = bf16[64,2688]{1,0:T(8,128)(2,1)S(1)} collective-permute-done((bf16[64,2688]{1,0:T(8,128)(2,1)}, bf16[64,2688]{1,0:T(8,128)(2,1)S(1)}, u32[]{:S(2)}, u32[]{:S(2)}) %collective-permute-start.18) | collective-permute-done | bytes 344096 | tf_op jit(solution)/shard_map/ppermute | solution.py:38
  174.4 3.3 %collective-permute-start.20 = (bf16[64,2688]{1,0:T(8,128)(2,1)S(1)}, bf16[64,2688]{1,0:T(8,128)(2,1)S(1)}, u32[]{:S(2)}, u32[]{:S(2)}) collective-permute-start(bf16[64,2688]{1,0:T(8,128)(2,1)S(1)} %collective-permute-done.18.refs_3_), channel_id=1, source_target_pairs={{0,56},{1,57},{2,58},{3,59},{4,60},{5,61},{6,62},{7,63},{8,0},{9,1... | collective-permute-start | bytes 1032200 | tf_op jit(solution)/shard_map/ppermute | solution.py:38
  177.8 5.7 %collective-permute-done.20.refs_5_ = bf16[64,2688]{1,0:T(8,128)(2,1)S(1)} collective-permute-done((bf16[64,2688]{1,0:T(8,128)(2,1)S(1)}, bf16[64,2688]{1,0:T(8,128)(2,1)S(1)}, u32[]{:S(2)}, u32[]{:S(2)}) %collective-permute-start.20) | collective-permute-done | bytes 344096 | tf_op jit(solution)/shard_map/ppermute | solution.py:38
  183.5 3.4 %collective-permute-start.23 = (bf16[64,2688]{1,0:T(8,128)(2,1)S(1)}, bf16[64,2688]{1,0:T(8,128)(2,1)S(1)}, u32[]{:S(2)}, u32[]{:S(2)}) collective-permute-start(bf16[64,2688]{1,0:T(8,128)(2,1)S(1)} %collective-permute-done.20.refs_5_), channel_id=1, source_target_pairs={{0,56},{1,57},{2,58},{3,59},{4,60},{5,61},{6,62},{7,63},{8,0},{9,1... | collective-permute-start | bytes 1032200 | tf_op jit(solution)/shard_map/ppermute | solution.py:38
  187.6 3.6 %dispatch.6 = (bf16[40,2560]{1,0:T(8,128)(2,1)}, bf16[40,2560]{1,0:T(8,128)(2,1)}, bf16[80,2560]{1,0:T(8,128)(2,1)}, bf16[80,2560]{1,0:T(8,128)(2,1)}, bf16[80,2560]{1,0:T(8,128)(2,1)}) custom-call(s32[8]{0:T(128)} %fusion.3.refs_0_, bf16[64,2688]{1,0:T(8,128)(2,1)} %get-tuple-element.61.refs_1_, bf16[64,2688]{1,0:T(8,128)(2,1)} %copy-done.15, ...), custom_call_target="tpu_custom_call" | custom-call | flops 1000 | bytes 1000 | tf_op jit(solution)/shard_map/dispatch/pallas_call | solution.py:139
  198.3 3.5 %collective-permute-done.24.refs_3_ = bf16[32,2688]{1,0:T(8,128)(2,1)S(1)} collective-permute-done((bf16[32,2688]{1,0:T(8,128)(2,1)S(1)}, bf16[32,2688]{1,0:T(8,128)(2,1)S(1)}, u32[]{:S(2)}, u32[]{:S(2)}) %collective-permute-start.24) | collective-permute-done | bytes 172064 | tf_op jit(solution)/shard_map/ppermute | solution.py:38
  201.9 2.6 dispatch.7
  208.7 5.5 %collective-permute-done.27.refs_4_ = bf16[80,2560]{1,0:T(8,128)(2,1)S(1)} collective-permute-done((bf16[80,2560]{1,0:T(8,128)(2,1)}, bf16[80,2560]{1,0:T(8,128)(2,1)S(1)}, u32[]{:S(2)}, u32[]{:S(2)}) %collective-permute-start.27) | collective-permute-done | bytes 409632 | tf_op jit(solution)/shard_map/ppermute | solution.py:38
  214.3 3.7 %collective-permute-start.28 = (bf16[160,2560]{1,0:T(8,128)(2,1)S(1)}, bf16[160,2560]{1,0:T(8,128)(2,1)S(1)}, u32[]{:S(2)}, u32[]{:S(2)}) collective-permute-start(bf16[160,2560]{1,0:T(8,128)(2,1)S(1)} %pad_maximum_fusion.1), channel_id=1, source_target_pairs={{0,1},{1,0},{2,3},{3,2},{4,5},{5,4},{6,7},{7,6},{8,9},{9,8},{10,11... | collective-permute-start | bytes 2457608 | tf_op jit(solution)/shard_map/ppermute | solution.py:38
  217.9 3.4 %collective-permute-done.29.refs_7_ = bf16[48,2560]{1,0:T(8,128)(2,1)S(1)} collective-permute-done((bf16[48,2560]{1,0:T(8,128)(2,1)}, bf16[48,2560]{1,0:T(8,128)(2,1)S(1)}, u32[]{:S(2)}, u32[]{:S(2)}) %collective-permute-start.29) | collective-permute-done | bytes 245792 | tf_op jit(solution)/shard_map/ppermute | solution.py:38
  221.5 3.1 %collective-permute-start.32 = (bf16[96,2560]{1,0:T(8,128)(2,1)S(1)}, bf16[96,2560]{1,0:T(8,128)(2,1)S(1)}, u32[]{:S(2)}, u32[]{:S(2)}) collective-permute-start(bf16[96,2560]{1,0:T(8,128)(2,1)S(1)} %pad_maximum_fusion.3), channel_id=1, source_target_pairs={{0,1},{1,0},{2,3},{3,2},{4,5},{5,4},{6,7},{7,6},{8,9},{9,8},{10,11... | collective-permute-start | bytes 1474568 | tf_op jit(solution)/shard_map/ppermute | solution.py:38
  226.1 10.4 %experts.3 = bf16[64,8,2560]{2,1,0:T(8,128)(2,1)S(1)} custom-call(s32[64]{0:T(128)S(1)} %fusion.1.refs_0_, bf16[40,2560]{1,0:T(8,128)(2,1)S(1)} %copy-done.1, bf16[80,2560]{1,0:T(8,128)(2,1)S(1)} %collective-permute-done.21.refs_2_, bf16[80,2560]{1,0:T(8,128)(2,1)S(1)} %collective-permute-done.26.refs_3_, ...), custom_call_target="tpu_custom_call" | custom-call | flops 1000 | bytes 1000 | tf_op jit(solution)/shard_map/experts/pallas_call | solution.py:216
  236.5 69.2 %all_to_all.11 = bf16[64,8,2560]{2,1,0:T(8,128)(2,1)} all-to-all(bf16[64,8,2560]{2,1,0:T(8,128)(2,1)S(1)} %experts.3), channel_id=1, replica_groups=mesh['segment'=4,'expert'=32,'dp'=2] {'expert','dp'}, dimensions={0} | all-to-all | bytes 5242880 | tf_op jit(solution)/shard_map/all_to_all | solution.py:277
  305.7 3.3 %combine.3 = bf16[2,64,2560]{2,1,0:T(8,128)(2,1)} custom-call(bf16[64,2560]{1,0:T(8,128)(2,1)} %get-tuple-element.59.refs_0_, bf16[64,512]{1,0:T(8,128)(2,1)} %get-tuple-element.60.refs_1_, bf16[512,2560]{1,0:T(8,128)(2,1)} %bitcast.22, bf16[1,64,2560]{2,1,0:T(8,128)(2,1)} %combine.2.refs_3_), custom_call_target="tpu_custom_call" | custom-call | flops 1000 | bytes 1000 | tf_op jit(solution)/shard_map/combine/pallas_call | solution.py:247
  (116 shorter events, 34.3 us)
Async XLA Ops:
  2.7 12.6 %collective-permute-start.1 = (bf16[64,2688]{1,0:T(8,128)(2,1)}, bf16[64,2688]{1,0:T(8,128)(2,1)S(1)}, u32[]{:S(2)}, u32[]{:S(2)}) collective-permute-start(bf16[64,2688]{1,0:T(8,128)(2,1)} %get-tuple-element.43.refs_1_), channel_id=1, source_target_pairs={{0,56},{1,57},{2,58},{3,59},{4,60},{5,61},{6,62},{7,63},{8,0},{9,1... | collective-permute-start | bytes 1032200 | tf_op jit(solution)/shard_map/ppermute | solution.py:38
  8.3 10.4 %collective-permute-start = (bf16[64,2688]{1,0:T(8,128)(2,1)}, bf16[64,2688]{1,0:T(8,128)(2,1)S(1)}, u32[]{:S(2)}, u32[]{:S(2)}) collective-permute-start(bf16[64,2688]{1,0:T(8,128)(2,1)} %get-tuple-element.43.refs_1_), channel_id=1, source_target_pairs={{0,8},{1,9},{2,10},{3,11},{4,12},{5,13},{6,14},{7,15},{8,16},{9,17... | collective-permute-start | bytes 1032200 | tf_op jit(solution)/shard_map/ppermute | solution.py:38
  15.3 9.1 %collective-permute-start.3 = (bf16[64,2688]{1,0:T(8,128)(2,1)S(1)}, bf16[64,2688]{1,0:T(8,128)(2,1)S(1)}, u32[]{:S(2)}, u32[]{:S(2)}) collective-permute-start(bf16[64,2688]{1,0:T(8,128)(2,1)S(1)} %collective-permute-done.1.refs_3_), channel_id=1, source_target_pairs={{0,56},{1,57},{2,58},{3,59},{4,60},{5,61},{6,62},{7,63},{8,0},{9,1... | collective-permute-start | bytes 1032200 | tf_op jit(solution)/shard_map/ppermute | solution.py:38
  18.6 9.2 %collective-permute-start.2 = (bf16[64,2688]{1,0:T(8,128)(2,1)S(1)}, bf16[64,2688]{1,0:T(8,128)(2,1)S(1)}, u32[]{:S(2)}, u32[]{:S(2)}) collective-permute-start(bf16[64,2688]{1,0:T(8,128)(2,1)S(1)} %collective-permute-done.refs_2_), channel_id=1, source_target_pairs={{0,8},{1,9},{2,10},{3,11},{4,12},{5,13},{6,14},{7,15},{8,16},{9,17... | collective-permute-start | bytes 1032200 | tf_op jit(solution)/shard_map/ppermute | solution.py:38
  24.4 12.8 %collective-permute-start.6 = (bf16[64,2688]{1,0:T(8,128)(2,1)S(1)}, bf16[64,2688]{1,0:T(8,128)(2,1)S(1)}, u32[]{:S(2)}, u32[]{:S(2)}) collective-permute-start(bf16[64,2688]{1,0:T(8,128)(2,1)S(1)} %collective-permute-done.3.refs_5_), channel_id=1, source_target_pairs={{0,56},{1,57},{2,58},{3,59},{4,60},{5,61},{6,62},{7,63},{8,0},{9,1... | collective-permute-start | bytes 1032200 | tf_op jit(solution)/shard_map/ppermute | solution.py:38
  27.8 12.0 %collective-permute-start.5 = (bf16[64,2688]{1,0:T(8,128)(2,1)S(1)}, bf16[64,2688]{1,0:T(8,128)(2,1)S(1)}, u32[]{:S(2)}, u32[]{:S(2)}) collective-permute-start(bf16[64,2688]{1,0:T(8,128)(2,1)S(1)} %collective-permute-done.2.refs_4_), channel_id=1, source_target_pairs={{0,8},{1,9},{2,10},{3,11},{4,12},{5,13},{6,14},{7,15},{8,16},{9,17... | collective-permute-start | bytes 1032200 | tf_op jit(solution)/shard_map/ppermute | solution.py:38
  32.2 17.3 %collective-permute-start.4 = (bf16[80,2560]{1,0:T(8,128)(2,1)}, bf16[80,2560]{1,0:T(8,128)(2,1)S(1)}, u32[]{:S(2)}, u32[]{:S(2)}) collective-permute-start(bf16[80,2560]{1,0:T(8,128)(2,1)} %get-tuple-element.45), channel_id=1, source_target_pairs={{0,2},{1,3},{2,4},{3,5},{4,6},{5,7},{6,0},{7,1},{8,10},{9,11},{10,... | collective-permute-start | bytes 1228808 | tf_op jit(solution)/shard_map/ppermute | solution.py:38
  33.5 18.4 %collective-permute-start.9 = (bf16[80,2560]{1,0:T(8,128)(2,1)}, bf16[80,2560]{1,0:T(8,128)(2,1)S(1)}, u32[]{:S(2)}, u32[]{:S(2)}) collective-permute-start(bf16[80,2560]{1,0:T(8,128)(2,1)} %get-tuple-element.50), channel_id=1, source_target_pairs={{0,4},{1,5},{2,6},{3,7},{4,0},{5,1},{6,2},{7,3},{8,12},{9,13},{10,... | collective-permute-start | bytes 1228808 | tf_op jit(solution)/shard_map/ppermute | solution.py:38
  36.1 18.3 %collective-permute-start.10 = (bf16[80,2560]{1,0:T(8,128)(2,1)}, bf16[80,2560]{1,0:T(8,128)(2,1)S(1)}, u32[]{:S(2)}, u32[]{:S(2)}) collective-permute-start(bf16[80,2560]{1,0:T(8,128)(2,1)} %get-tuple-element.52), channel_id=1, source_target_pairs={{0,6},{1,7},{2,0},{3,1},{4,2},{5,3},{6,4},{7,5},{8,14},{9,15},{10,... | collective-permute-start | bytes 1228808 | tf_op jit(solution)/shard_map/ppermute | solution.py:38
  37.2 5.0 %collective-permute-start.8 = (bf16[32,2688]{1,0:T(8,128)(2,1)S(1)}, bf16[32,2688]{1,0:T(8,128)(2,1)S(1)}, u32[]{:S(2)}, u32[]{:S(2)}) collective-permute-start(bf16[32,2688]{1,0:T(8,128)(2,1)S(1)} %slice.49), channel_id=1, source_target_pairs={{0,56},{1,57},{2,58},{3,59},{4,60},{5,61},{6,62},{7,63},{8,0},{9,1... | collective-permute-start | bytes 516104 | tf_op jit(solution)/shard_map/ppermute | solution.py:38
  39.9 5.8 %collective-permute-start.7 = (bf16[32,2688]{1,0:T(8,128)(2,1)S(1)}, bf16[32,2688]{1,0:T(8,128)(2,1)S(1)}, u32[]{:S(2)}, u32[]{:S(2)}) collective-permute-start(bf16[32,2688]{1,0:T(8,128)(2,1)S(1)} %slice.48), channel_id=1, source_target_pairs={{0,8},{1,9},{2,10},{3,11},{4,12},{5,13},{6,14},{7,15},{8,16},{9,17... | collective-permute-start | bytes 516104 | tf_op jit(solution)/shard_map/ppermute | solution.py:38
  48.3 10.9 %collective-permute-start.12 = (bf16[48,2560]{1,0:T(8,128)(2,1)}, bf16[48,2560]{1,0:T(8,128)(2,1)S(1)}, u32[]{:S(2)}, u32[]{:S(2)}) collective-permute-start(bf16[48,2560]{1,0:T(8,128)(2,1)} %get-tuple-element.55), channel_id=1, source_target_pairs={{0,2},{1,3},{2,4},{3,5},{4,6},{5,7},{6,0},{7,1},{8,10},{9,11},{10,... | collective-permute-start | bytes 737288 | tf_op jit(solution)/shard_map/ppermute | solution.py:38
  48.5 13.6 %collective-permute-start.13 = (bf16[48,2560]{1,0:T(8,128)(2,1)}, bf16[48,2560]{1,0:T(8,128)(2,1)S(1)}, u32[]{:S(2)}, u32[]{:S(2)}) collective-permute-start(bf16[48,2560]{1,0:T(8,128)(2,1)} %get-tuple-element.56), channel_id=1, source_target_pairs={{0,4},{1,5},{2,6},{3,7},{4,0},{5,1},{6,2},{7,3},{8,12},{9,13},{10,... | collective-permute-start | bytes 737288 | tf_op jit(solution)/shard_map/ppermute | solution.py:38
  49.5 13.2 %collective-permute-start.14 = (bf16[48,2560]{1,0:T(8,128)(2,1)}, bf16[48,2560]{1,0:T(8,128)(2,1)S(1)}, u32[]{:S(2)}, u32[]{:S(2)}) collective-permute-start(bf16[48,2560]{1,0:T(8,128)(2,1)} %get-tuple-element.57), channel_id=1, source_target_pairs={{0,6},{1,7},{2,0},{3,1},{4,2},{5,3},{6,4},{7,5},{8,14},{9,15},{10,... | collective-permute-start | bytes 737288 | tf_op jit(solution)/shard_map/ppermute | solution.py:38
  54.6 13.4 %collective-permute-start.11 = (bf16[160,2560]{1,0:T(8,128)(2,1)S(1)}, bf16[160,2560]{1,0:T(8,128)(2,1)S(1)}, u32[]{:S(2)}, u32[]{:S(2)}) collective-permute-start(bf16[160,2560]{1,0:T(8,128)(2,1)S(1)} %pad_maximum_fusion), channel_id=1, source_target_pairs={{0,1},{1,0},{2,3},{3,2},{4,5},{5,4},{6,7},{7,6},{8,9},{9,8},{10,11... | collective-permute-start | bytes 2457608 | tf_op jit(solution)/shard_map/ppermute | solution.py:38
  62.8 5.3 %collective-permute-start.15 = (bf16[96,2560]{1,0:T(8,128)(2,1)S(1)}, bf16[96,2560]{1,0:T(8,128)(2,1)S(1)}, u32[]{:S(2)}, u32[]{:S(2)}) collective-permute-start(bf16[96,2560]{1,0:T(8,128)(2,1)S(1)} %pad_maximum_fusion.2), channel_id=1, source_target_pairs={{0,1},{1,0},{2,3},{3,2},{4,5},{5,4},{6,7},{7,6},{8,9},{9,8},{10,11... | collective-permute-start | bytes 1474568 | tf_op jit(solution)/shard_map/ppermute | solution.py:38
  151.0 11.0 %collective-permute-start.16 = (bf16[64,2560]{1,0:T(8,128)(2,1)}, bf16[64,2560]{1,0:T(8,128)(2,1)S(1)}, u32[]{:S(2)}, u32[]{:S(2)}) collective-permute-start(bf16[64,2560]{1,0:T(8,128)(2,1)} %bitcast.28), channel_id=1, source_target_pairs={{0,64},{64,128},{128,192},{1,65},{65,129},{129,193},{2,66},{66,130... | collective-permute-start | bytes 983048 | tf_op jit(solution)/shard_map/ppermute | solution.py:302
  165.3 9.1 %collective-permute-start.18 = (bf16[64,2688]{1,0:T(8,128)(2,1)}, bf16[64,2688]{1,0:T(8,128)(2,1)S(1)}, u32[]{:S(2)}, u32[]{:S(2)}) collective-permute-start(bf16[64,2688]{1,0:T(8,128)(2,1)} %get-tuple-element.61.refs_1_), channel_id=1, source_target_pairs={{0,56},{1,57},{2,58},{3,59},{4,60},{5,61},{6,62},{7,63},{8,0},{9,1... | collective-permute-start | bytes 1032200 | tf_op jit(solution)/shard_map/ppermute | solution.py:38
  167.5 10.3 %collective-permute-start.17 = (bf16[64,2688]{1,0:T(8,128)(2,1)}, bf16[64,2688]{1,0:T(8,128)(2,1)S(1)}, u32[]{:S(2)}, u32[]{:S(2)}) collective-permute-start(bf16[64,2688]{1,0:T(8,128)(2,1)} %get-tuple-element.61.refs_1_), channel_id=1, source_target_pairs={{0,8},{1,9},{2,10},{3,11},{4,12},{5,13},{6,14},{7,15},{8,16},{9,17... | collective-permute-start | bytes 1032200 | tf_op jit(solution)/shard_map/ppermute | solution.py:38
  174.4 9.0 %collective-permute-start.20 = (bf16[64,2688]{1,0:T(8,128)(2,1)S(1)}, bf16[64,2688]{1,0:T(8,128)(2,1)S(1)}, u32[]{:S(2)}, u32[]{:S(2)}) collective-permute-start(bf16[64,2688]{1,0:T(8,128)(2,1)S(1)} %collective-permute-done.18.refs_3_), channel_id=1, source_target_pairs={{0,56},{1,57},{2,58},{3,59},{4,60},{5,61},{6,62},{7,63},{8,0},{9,1... | collective-permute-start | bytes 1032200 | tf_op jit(solution)/shard_map/ppermute | solution.py:38
  177.8 9.1 %collective-permute-start.19 = (bf16[64,2688]{1,0:T(8,128)(2,1)S(1)}, bf16[64,2688]{1,0:T(8,128)(2,1)S(1)}, u32[]{:S(2)}, u32[]{:S(2)}) collective-permute-start(bf16[64,2688]{1,0:T(8,128)(2,1)S(1)} %collective-permute-done.17.refs_2_), channel_id=1, source_target_pairs={{0,8},{1,9},{2,10},{3,11},{4,12},{5,13},{6,14},{7,15},{8,16},{9,17... | collective-permute-start | bytes 1032200 | tf_op jit(solution)/shard_map/ppermute | solution.py:38
  183.5 10.4 %collective-permute-start.23 = (bf16[64,2688]{1,0:T(8,128)(2,1)S(1)}, bf16[64,2688]{1,0:T(8,128)(2,1)S(1)}, u32[]{:S(2)}, u32[]{:S(2)}) collective-permute-start(bf16[64,2688]{1,0:T(8,128)(2,1)S(1)} %collective-permute-done.20.refs_5_), channel_id=1, source_target_pairs={{0,56},{1,57},{2,58},{3,59},{4,60},{5,61},{6,62},{7,63},{8,0},{9,1... | collective-permute-start | bytes 1032200 | tf_op jit(solution)/shard_map/ppermute | solution.py:38
  186.9 9.1 %collective-permute-start.22 = (bf16[64,2688]{1,0:T(8,128)(2,1)S(1)}, bf16[64,2688]{1,0:T(8,128)(2,1)S(1)}, u32[]{:S(2)}, u32[]{:S(2)}) collective-permute-start(bf16[64,2688]{1,0:T(8,128)(2,1)S(1)} %collective-permute-done.19.refs_4_), channel_id=1, source_target_pairs={{0,8},{1,9},{2,10},{3,11},{4,12},{5,13},{6,14},{7,15},{8,16},{9,17... | collective-permute-start | bytes 1032200 | tf_op jit(solution)/shard_map/ppermute | solution.py:38
  191.2 15.3 %collective-permute-start.21 = (bf16[80,2560]{1,0:T(8,128)(2,1)}, bf16[80,2560]{1,0:T(8,128)(2,1)S(1)}, u32[]{:S(2)}, u32[]{:S(2)}) collective-permute-start(bf16[80,2560]{1,0:T(8,128)(2,1)} %get-tuple-element.63), channel_id=1, source_target_pairs={{0,2},{1,3},{2,4},{3,5},{4,6},{5,7},{6,0},{7,1},{8,10},{9,11},{10,... | collective-permute-start | bytes 1228808 | tf_op jit(solution)/shard_map/ppermute | solution.py:38
  191.2 17.4 %collective-permute-start.26 = (bf16[80,2560]{1,0:T(8,128)(2,1)}, bf16[80,2560]{1,0:T(8,128)(2,1)S(1)}, u32[]{:S(2)}, u32[]{:S(2)}) collective-permute-start(bf16[80,2560]{1,0:T(8,128)(2,1)} %get-tuple-element.68), channel_id=1, source_target_pairs={{0,4},{1,5},{2,6},{3,7},{4,0},{5,1},{6,2},{7,3},{8,12},{9,13},{10,... | collective-permute-start | bytes 1228808 | tf_op jit(solution)/shard_map/ppermute | solution.py:38
  191.5 22.7 %collective-permute-start.27 = (bf16[80,2560]{1,0:T(8,128)(2,1)}, bf16[80,2560]{1,0:T(8,128)(2,1)S(1)}, u32[]{:S(2)}, u32[]{:S(2)}) collective-permute-start(bf16[80,2560]{1,0:T(8,128)(2,1)} %get-tuple-element.70), channel_id=1, source_target_pairs={{0,6},{1,7},{2,0},{3,1},{4,2},{5,3},{6,4},{7,5},{8,14},{9,15},{10,... | collective-permute-start | bytes 1228808 | tf_op jit(solution)/shard_map/ppermute | solution.py:38
  196.0 5.8 %collective-permute-start.24 = (bf16[32,2688]{1,0:T(8,128)(2,1)S(1)}, bf16[32,2688]{1,0:T(8,128)(2,1)S(1)}, u32[]{:S(2)}, u32[]{:S(2)}) collective-permute-start(bf16[32,2688]{1,0:T(8,128)(2,1)S(1)} %slice.56), channel_id=1, source_target_pairs={{0,8},{1,9},{2,10},{3,11},{4,12},{5,13},{6,14},{7,15},{8,16},{9,17... | collective-permute-start | bytes 516104 | tf_op jit(solution)/shard_map/ppermute | solution.py:38
  204.5 16.9 %collective-permute-start.29 = (bf16[48,2560]{1,0:T(8,128)(2,1)}, bf16[48,2560]{1,0:T(8,128)(2,1)S(1)}, u32[]{:S(2)}, u32[]{:S(2)}) collective-permute-start(bf16[48,2560]{1,0:T(8,128)(2,1)} %get-tuple-element.73), channel_id=1, source_target_pairs={{0,2},{1,3},{2,4},{3,5},{4,6},{5,7},{6,0},{7,1},{8,10},{9,11},{10,... | collective-permute-start | bytes 737288 | tf_op jit(solution)/shard_map/ppermute | solution.py:38
  204.9 16.5 %collective-permute-start.30 = (bf16[48,2560]{1,0:T(8,128)(2,1)}, bf16[48,2560]{1,0:T(8,128)(2,1)S(1)}, u32[]{:S(2)}, u32[]{:S(2)}) collective-permute-start(bf16[48,2560]{1,0:T(8,128)(2,1)} %get-tuple-element.74), channel_id=1, source_target_pairs={{0,4},{1,5},{2,6},{3,7},{4,0},{5,1},{6,2},{7,3},{8,12},{9,13},{10,... | collective-permute-start | bytes 737288 | tf_op jit(solution)/shard_map/ppermute | solution.py:38
  206.5 14.9 %collective-permute-start.31 = (bf16[48,2560]{1,0:T(8,128)(2,1)}, bf16[48,2560]{1,0:T(8,128)(2,1)S(1)}, u32[]{:S(2)}, u32[]{:S(2)}) collective-permute-start(bf16[48,2560]{1,0:T(8,128)(2,1)} %get-tuple-element.75), channel_id=1, source_target_pairs={{0,6},{1,7},{2,0},{3,1},{4,2},{5,3},{6,4},{7,5},{8,14},{9,15},{10,... | collective-permute-start | bytes 737288 | tf_op jit(solution)/shard_map/ppermute | solution.py:38
  214.3 11.8 %collective-permute-start.28 = (bf16[160,2560]{1,0:T(8,128)(2,1)S(1)}, bf16[160,2560]{1,0:T(8,128)(2,1)S(1)}, u32[]{:S(2)}, u32[]{:S(2)}) collective-permute-start(bf16[160,2560]{1,0:T(8,128)(2,1)S(1)} %pad_maximum_fusion.1), channel_id=1, source_target_pairs={{0,1},{1,0},{2,3},{3,2},{4,5},{5,4},{6,7},{7,6},{8,9},{9,8},{10,11... | collective-permute-start | bytes 2457608 | tf_op jit(solution)/shard_map/ppermute | solution.py:38
  221.5 4.6 %collective-permute-start.32 = (bf16[96,2560]{1,0:T(8,128)(2,1)S(1)}, bf16[96,2560]{1,0:T(8,128)(2,1)S(1)}, u32[]{:S(2)}, u32[]{:S(2)}) collective-permute-start(bf16[96,2560]{1,0:T(8,128)(2,1)S(1)} %pad_maximum_fusion.3), channel_id=1, source_target_pairs={{0,1},{1,0},{2,3},{3,2},{4,5},{5,4},{6,7},{7,6},{8,9},{9,8},{10,11... | collective-permute-start | bytes 1474568 | tf_op jit(solution)/shard_map/ppermute | solution.py:38
  (25 other events, 243.9 us)
where the time goes:
time: 309 us
  blocking collectives  139 us (45%)
  waiting for transfers between devices  65.6 us (21%)
  starting transfers between devices  56.9 us (18%)
  Pallas kernels  44.9 us (15%)
    all_to_all x2, blocking collectives, section(): lax.all_to_all(outputs, GROUP, split_axis=0, concat_axis=0, tiled=True)  139 us
    ppermute x32, waiting for transfers between devices, move(): return lax.ppermute(value, GROUP, pairs)  55.8 us
    ppermute x32, starting transfers between devices, move(): return lax.ppermute(value, GROUP, pairs)  55.6 us
    pallas_call x2, Pallas kernels, run_experts(): pl.pallas_call(lambda *refs: experts_kernel(len(groups), *refs), out_shap...  20.7 us
    pallas_call x4, Pallas kernels, dispatch(): pl.pallas_call(lambda *refs: dispatch_kernel(block, len(packed), *refs),...  12.4 us
    ppermute x1, waiting for transfers between devices, shards(): lax.ppermute(results[-1][0], 'segment', [(i, i + 1) for i in range(count...  9.75 us
    pallas_call x2, Pallas kernels, combine(): pl.pallas_call(lambda *refs: combine_kernel(len(results), *refs), out_sha...  6.5 us
  transfers between devices with their start and end apart: 33, of which 17 were waited for; matrix products, arithmetic and copies ran while one was open for 0% of the time, Pallas kernels for 4%

commit v1 on v0

--- a/solution.py
+++ b/solution.py
@@ -48,6 +48,10 @@
 
 def along_z(value, steps):
     return move(value, lambda z, y, core: (z + steps, y, core))
+
+
+def held_close(value):
+    return pltpu.with_memory_space_constraint(value, pltpu.VMEM)
 
 
 def after(value, *others):
@@ -196,15 +200,12 @@
         hidden_ref[:, cols] = (gate / (1.0 + jnp.exp(-gate)) * upper_ref[:, cols]).astype(jnp.bfloat16)
     last.wait()
 
-    def give(index, carry):
-        cols = pl.ds(pl.multiple_of(index * 512, 512), 512)
-        result = dot(hidden_ref[...], down_ref[:, cols])
+    hidden = hidden_ref[...]
+    for cols in column_tiles(width, 512):
+        result = dot(hidden, down_ref[:, cols])
         for place in range(out_ref.shape[0]):
             piece = result[place * CAP : (place + 1) * CAP].astype(jnp.bfloat16)
             out_ref[pl.ds(places_ref[place], 1), :, cols] = piece[None]
-        return carry
-
-    lax.fori_loop(0, width // 512, give, 0)
 
 
 def run_experts(groups, places, w_gate, w_up, w_down):
@@ -264,18 +265,18 @@
     for _ in range(2):
         below.append(along_z(below[-1], 1))
         above.append(along_z(above[-1], -1))
-    near_rows = dispatch(ids, [packed, below[1], above[1], below[2], above[2]], tokens)
+    near = [packed] + [held_close(value) for value in (below[1], above[1], below[2], above[2])]
+    near_rows = dispatch(ids, near, tokens)
     below.append(along_z(below[2], 1))
     above.append(along_z(above[2], -1))
     third = after(below[3], near_rows[0]), after(above[3], near_rows[0])
     far = [below[3], above[3], along_z(third[0][:part], 1), along_z(third[1][part:], -1)]
-    far = far[:2] + [pltpu.with_memory_space_constraint(value, pltpu.VMEM) for value in far[2:]]
-    far_rows = dispatch(ids, far, tokens)
+    far_rows = dispatch(ids, [held_close(value) for value in far], tokens)
     own, other, there = travelled(near_rows)
     near_there = own, other, [after(value, far_rows[0]) for value in there]
     outputs = run_experts([near_there, travelled(far_rows)], places, w_gate, w_up, w_down)
     landed = lax.all_to_all(outputs, GROUP, split_axis=0, concat_axis=0, tiled=True)
-    return landed.reshape(-1, landed.shape[-1])
+    return held_close(landed.reshape(-1, landed.shape[-1]))
 
 
 def shards(entering, fresh, w_gate, w_up, w_down, router, gain, routes):
@@ -299,7 +300,7 @@
         if index == 0:
             first, arrived, other = never, entering[0], entering[0]
         else:
-            arrived = lax.ppermute(results[-1][0], "segment", [(i, i + 1) for i in range(count - 1)])
+            arrived = held_close(lax.ppermute(results[-1][0], "segment", [(i, i + 1) for i in range(count - 1)]))
             first, other = at_start, fresh[index - 1]
         current, packed, weights = prepare(index, first, arrived, other, gain, router_rows, picks)
         landed = section(packed, ids, places, w_gate, w_up, w_down)

time: 309 us -> 304 us (0.984)
  Pallas kernels: 44.9 us -> 40 us
where the time goes in v1:
time: 304 us
  blocking collectives  139 us (46%)
  waiting for transfers between devices  65.3 us (21%)
  starting transfers between devices  57.9 us (19%)
  Pallas kernels  40 us (13%)
    all_to_all x2, blocking collectives, section(): lax.all_to_all(outputs, GROUP, split_axis=0, concat_axis=0, tiled=True)  139 us
    ppermute x32, starting transfers between devices, move(): return lax.ppermute(value, GROUP, pairs)  56.7 us
    ppermute x32, waiting for transfers between devices, move(): return lax.ppermute(value, GROUP, pairs)  55.5 us
    pallas_call x2, Pallas kernels, run_experts(): pl.pallas_call(lambda *refs: experts_kernel(len(groups), *refs), out_shap...  19.4 us
    pallas_call x4, Pallas kernels, dispatch(): pl.pallas_call(lambda *refs: dispatch_kernel(block, len(packed), *refs),...  10.8 us
    ppermute x1, waiting for transfers between devices, shards(): lax.ppermute(results[-1][0], 'segment', [(i, i + 1) for i in range(count...  9.75 us
  transfers between devices with their start and end apart: 33, of which 17 were waited for; matrix products, arithmetic and copies ran while one was open for 0% of the time, Pallas kernels for 4%

profile of v1, /device:TPU:7, one launch (start us, length us, event | category | flops | bytes accessed | tf_op | source)
XLA Modules:
  0.0 303.9 jit_solution(11730970904511861136)
XLA Ops:
  0.0 2.5 prepare.2
  2.5 5.6 %collective-permute-start.1 = (bf16[64,2688]{1,0:T(8,128)(2,1)}, bf16[64,2688]{1,0:T(8,128)(2,1)S(1)}, u32[]{:S(2)}, u32[]{:S(2)}) collective-permute-start(bf16[64,2688]{1,0:T(8,128)(2,1)} %get-tuple-element.43.refs_1_), channel_id=1, source_target_pairs={{0,56},{1,57},{2,58},{3,59},{4,60},{5,61},{6,62},{7,63},{8,0},{9,1... | collective-permute-start | bytes 1032200 | tf_op jit(solution)/shard_map/ppermute | solution.py:38
  8.1 7.0 %collective-permute-done.1.refs_3_ = bf16[64,2688]{1,0:T(8,128)(2,1)S(1)} collective-permute-done((bf16[64,2688]{1,0:T(8,128)(2,1)}, bf16[64,2688]{1,0:T(8,128)(2,1)S(1)}, u32[]{:S(2)}, u32[]{:S(2)}) %collective-permute-start.1) | collective-permute-done | bytes 344096 | tf_op jit(solution)/shard_map/ppermute | solution.py:38
  15.2 3.3 %collective-permute-start.3 = (bf16[64,2688]{1,0:T(8,128)(2,1)S(1)}, bf16[64,2688]{1,0:T(8,128)(2,1)S(1)}, u32[]{:S(2)}, u32[]{:S(2)}) collective-permute-start(bf16[64,2688]{1,0:T(8,128)(2,1)S(1)} %collective-permute-done.1.refs_3_), channel_id=1, source_target_pairs={{0,56},{1,57},{2,58},{3,59},{4,60},{5,61},{6,62},{7,63},{8,0},{9,1... | collective-permute-start | bytes 1032200 | tf_op jit(solution)/shard_map/ppermute | solution.py:38
  18.5 5.8 %collective-permute-done.3.refs_5_ = bf16[64,2688]{1,0:T(8,128)(2,1)S(1)} collective-permute-done((bf16[64,2688]{1,0:T(8,128)(2,1)S(1)}, bf16[64,2688]{1,0:T(8,128)(2,1)S(1)}, u32[]{:S(2)}, u32[]{:S(2)}) %collective-permute-start.3) | collective-permute-done | bytes 344096 | tf_op jit(solution)/shard_map/ppermute | solution.py:38
  24.3 3.4 %collective-permute-start.6 = (bf16[64,2688]{1,0:T(8,128)(2,1)S(1)}, bf16[64,2688]{1,0:T(8,128)(2,1)S(1)}, u32[]{:S(2)}, u32[]{:S(2)}) collective-permute-start(bf16[64,2688]{1,0:T(8,128)(2,1)S(1)} %collective-permute-done.3.refs_5_), channel_id=1, source_target_pairs={{0,56},{1,57},{2,58},{3,59},{4,60},{5,61},{6,62},{7,63},{8,0},{9,1... | collective-permute-start | bytes 1032200 | tf_op jit(solution)/shard_map/ppermute | solution.py:38
  28.2 3.2 %dispatch.4 = (bf16[40,2560]{1,0:T(8,128)(2,1)}, bf16[40,2560]{1,0:T(8,128)(2,1)}, bf16[80,2560]{1,0:T(8,128)(2,1)}, bf16[80,2560]{1,0:T(8,128)(2,1)}, bf16[80,2560]{1,0:T(8,128)(2,1)}) custom-call(s32[8]{0:T(128)} %fusion.3.refs_0_, bf16[64,2688]{1,0:T(8,128)(2,1)} %get-tuple-element.43.refs_1_, bf16[64,2688]{1,0:T(8,128)(2,1)S(1)} %collective-permute-done.refs_2_, ...), custom_call_target="tpu_custom_call" | custom-call | flops 1000 | bytes 1000 | tf_op jit(solution)/shard_map/dispatch/pallas_call | solution.py:143
  32.8 2.6 collective-permute-start.9
  36.5 2.7 collective-permute-start.8
  41.6 3.5 %collective-permute-done.7.refs_3_ = bf16[32,2688]{1,0:T(8,128)(2,1)S(1)} collective-permute-done((bf16[32,2688]{1,0:T(8,128)(2,1)S(1)}, bf16[32,2688]{1,0:T(8,128)(2,1)S(1)}, u32[]{:S(2)}, u32[]{:S(2)}) %collective-permute-start.7) | collective-permute-done | bytes 172064 | tf_op jit(solution)/shard_map/ppermute | solution.py:38
  51.2 2.5 collective-permute-done.10.refs_4_
  53.9 4.8 %collective-permute-start.11 = (bf16[160,2560]{1,0:T(8,128)(2,1)S(1)}, bf16[160,2560]{1,0:T(8,128)(2,1)S(1)}, u32[]{:S(2)}, u32[]{:S(2)}) collective-permute-start(bf16[160,2560]{1,0:T(8,128)(2,1)S(1)} %pad_maximum_fusion), channel_id=1, source_target_pairs={{0,1},{1,0},{2,3},{3,2},{4,5},{5,4},{6,7},{7,6},{8,9},{9,8},{10,11... | collective-permute-start | bytes 2457608 | tf_op jit(solution)/shard_map/ppermute | solution.py:38
  58.7 2.8 collective-permute-done.13.refs_8_
  62.2 3.5 %collective-permute-start.15 = (bf16[96,2560]{1,0:T(8,128)(2,1)S(1)}, bf16[96,2560]{1,0:T(8,128)(2,1)S(1)}, u32[]{:S(2)}, u32[]{:S(2)}) collective-permute-start(bf16[96,2560]{1,0:T(8,128)(2,1)S(1)} %pad_maximum_fusion.2), channel_id=1, source_target_pairs={{0,1},{1,0},{2,3},{3,2},{4,5},{5,4},{6,7},{7,6},{8,9},{9,8},{10,11... | collective-permute-start | bytes 1474568 | tf_op jit(solution)/shard_map/ppermute | solution.py:38
  67.2 9.7 %experts.2 = bf16[64,8,2560]{2,1,0:T(8,128)(2,1)S(1)} custom-call(s32[64]{0:T(128)S(1)} %fusion.1.refs_0_, bf16[40,2560]{1,0:T(8,128)(2,1)S(1)} %copy-done, bf16[80,2560]{1,0:T(8,128)(2,1)S(1)} %collective-permute-done.4.refs_2_, bf16[80,2560]{1,0:T(8,128)(2,1)S(1)} %collective-permute-done.9.refs_3_, bf16[80,2560]{1,0:T(8,128)(2,1)S(1)} %collective-permute-done.10.refs_4_, ...), custom_call_target="tpu_custom_call" | custom-call | flops 1000 | bytes 1000 | tf_op jit(solution)/shard_map/experts/pallas_call | solution.py:217
  76.9 69.5 %all_to_all.10 = bf16[64,8,2560]{2,1,0:T(8,128)(2,1)S(1)} all-to-all(bf16[64,8,2560]{2,1,0:T(8,128)(2,1)S(1)} %experts.2), channel_id=1, replica_groups=mesh['segment'=4,'expert'=32,'dp'=2] {'expert','dp'}, dimensions={0} | all-to-all | bytes 5242880 | tf_op jit(solution)/shard_map/all_to_all | solution.py:278
  150.0 9.7 %collective-permute-done.16.refs_1_ = bf16[64,2560]{1,0:T(8,128)(2,1)S(1)} collective-permute-done((bf16[64,2560]{1,0:T(8,128)(2,1)}, bf16[64,2560]{1,0:T(8,128)(2,1)S(1)}, u32[]{:S(2)}, u32[]{:S(2)}) %collective-permute-start.16) | collective-permute-done | bytes 327712 | tf_op jit(solution)/shard_map/ppermute | solution.py:303
  159.8 2.5 prepare.3
  164.4 7.0 %collective-permute-done.18.refs_3_ = bf16[64,2688]{1,0:T(8,128)(2,1)S(1)} collective-permute-done((bf16[64,2688]{1,0:T(8,128)(2,1)}, bf16[64,2688]{1,0:T(8,128)(2,1)S(1)}, u32[]{:S(2)}, u32[]{:S(2)}) %collective-permute-start.18) | collective-permute-done | bytes 344096 | tf_op jit(solution)/shard_map/ppermute | solution.py:38
  171.4 3.3 %collective-permute-start.20 = (bf16[64,2688]{1,0:T(8,128)(2,1)S(1)}, bf16[64,2688]{1,0:T(8,128)(2,1)S(1)}, u32[]{:S(2)}, u32[]{:S(2)}) collective-permute-start(bf16[64,2688]{1,0:T(8,128)(2,1)S(1)} %collective-permute-done.18.refs_3_), channel_id=1, source_target_pairs={{0,56},{1,57},{2,58},{3,59},{4,60},{5,61},{6,62},{7,63},{8,0},{9,1... | collective-permute-start | bytes 1032200 | tf_op jit(solution)/shard_map/ppermute | solution.py:38
  174.7 5.7 %collective-permute-done.20.refs_5_ = bf16[64,2688]{1,0:T(8,128)(2,1)S(1)} collective-permute-done((bf16[64,2688]{1,0:T(8,128)(2,1)S(1)}, bf16[64,2688]{1,0:T(8,128)(2,1)S(1)}, u32[]{:S(2)}, u32[]{:S(2)}) %collective-permute-start.20) | collective-permute-done | bytes 344096 | tf_op jit(solution)/shard_map/ppermute | solution.py:38
  180.4 3.4 %collective-permute-start.23 = (bf16[64,2688]{1,0:T(8,128)(2,1)S(1)}, bf16[64,2688]{1,0:T(8,128)(2,1)S(1)}, u32[]{:S(2)}, u32[]{:S(2)}) collective-permute-start(bf16[64,2688]{1,0:T(8,128)(2,1)S(1)} %collective-permute-done.20.refs_5_), channel_id=1, source_target_pairs={{0,56},{1,57},{2,58},{3,59},{4,60},{5,61},{6,62},{7,63},{8,0},{9,1... | collective-permute-start | bytes 1032200 | tf_op jit(solution)/shard_map/ppermute | solution.py:38
  183.8 3.2 %dispatch.6 = (bf16[40,2560]{1,0:T(8,128)(2,1)}, bf16[40,2560]{1,0:T(8,128)(2,1)}, bf16[80,2560]{1,0:T(8,128)(2,1)}, bf16[80,2560]{1,0:T(8,128)(2,1)}, bf16[80,2560]{1,0:T(8,128)(2,1)}) custom-call(s32[8]{0:T(128)} %fusion.3.refs_0_, bf16[64,2688]{1,0:T(8,128)(2,1)} %get-tuple-element.61.refs_1_, bf16[64,2688]{1,0:T(8,128)(2,1)S(1)} %collective-permute-done.17.refs_2_, ...), custom_call_target="tpu_custom_call" | custom-call | flops 1000 | bytes 1000 | tf_op jit(solution)/shard_map/dispatch/pallas_call | solution.py:143
  189.7 2.7 collective-permute-start.25
  194.8 3.5 %collective-permute-done.24.refs_3_ = bf16[32,2688]{1,0:T(8,128)(2,1)S(1)} collective-permute-done((bf16[32,2688]{1,0:T(8,128)(2,1)S(1)}, bf16[32,2688]{1,0:T(8,128)(2,1)S(1)}, u32[]{:S(2)}, u32[]{:S(2)}) %collective-permute-start.24) | collective-permute-done | bytes 172064 | tf_op jit(solution)/shard_map/ppermute | solution.py:38
  204.7 5.2 %collective-permute-done.27.refs_4_ = bf16[80,2560]{1,0:T(8,128)(2,1)S(1)} collective-permute-done((bf16[80,2560]{1,0:T(8,128)(2,1)}, bf16[80,2560]{1,0:T(8,128)(2,1)S(1)}, u32[]{:S(2)}, u32[]{:S(2)}) %collective-permute-start.27) | collective-permute-done | bytes 409632 | tf_op jit(solution)/shard_map/ppermute | solution.py:38
  210.1 3.9 %collective-permute-start.28 = (bf16[160,2560]{1,0:T(8,128)(2,1)S(1)}, bf16[160,2560]{1,0:T(8,128)(2,1)S(1)}, u32[]{:S(2)}, u32[]{:S(2)}) collective-permute-start(bf16[160,2560]{1,0:T(8,128)(2,1)S(1)} %pad_maximum_fusion.1), channel_id=1, source_target_pairs={{0,1},{1,0},{2,3},{3,2},{4,5},{5,4},{6,7},{7,6},{8,9},{9,8},{10,11... | collective-permute-start | bytes 2457608 | tf_op jit(solution)/shard_map/ppermute | solution.py:38
  214.0 3.2 %collective-permute-done.29.refs_7_ = bf16[48,2560]{1,0:T(8,128)(2,1)S(1)} collective-permute-done((bf16[48,2560]{1,0:T(8,128)(2,1)}, bf16[48,2560]{1,0:T(8,128)(2,1)S(1)}, u32[]{:S(2)}, u32[]{:S(2)}) %collective-permute-start.29) | collective-permute-done | bytes 245792 | tf_op jit(solution)/shard_map/ppermute | solution.py:38
  217.3 3.1 %collective-permute-start.32 = (bf16[96,2560]{1,0:T(8,128)(2,1)S(1)}, bf16[96,2560]{1,0:T(8,128)(2,1)S(1)}, u32[]{:S(2)}, u32[]{:S(2)}) collective-permute-start(bf16[96,2560]{1,0:T(8,128)(2,1)S(1)} %pad_maximum_fusion.3), channel_id=1, source_target_pairs={{0,1},{1,0},{2,3},{3,2},{4,5},{5,4},{6,7},{7,6},{8,9},{9,8},{10,11... | collective-permute-start | bytes 1474568 | tf_op jit(solution)/shard_map/ppermute | solution.py:38
  221.9 9.7 %experts.3 = bf16[64,8,2560]{2,1,0:T(8,128)(2,1)S(1)} custom-call(s32[64]{0:T(128)S(1)} %fusion.1.refs_0_, bf16[40,2560]{1,0:T(8,128)(2,1)S(1)} %copy-done.1, bf16[80,2560]{1,0:T(8,128)(2,1)S(1)} %collective-permute-done.21.refs_2_, bf16[80,2560]{1,0:T(8,128)(2,1)S(1)} %collective-permute-done.26.refs_3_, ...), custom_call_target="tpu_custom_call" | custom-call | flops 1000 | bytes 1000 | tf_op jit(solution)/shard_map/experts/pallas_call | solution.py:217
  231.6 69.8 %all_to_all.11 = bf16[64,8,2560]{2,1,0:T(8,128)(2,1)S(1)} all-to-all(bf16[64,8,2560]{2,1,0:T(8,128)(2,1)S(1)} %experts.3), channel_id=1, replica_groups=mesh['segment'=4,'expert'=32,'dp'=2] {'expert','dp'}, dimensions={0} | all-to-all | bytes 5242880 | tf_op jit(solution)/shard_map/all_to_all | solution.py:278
  301.4 2.5 combine.3
  (90 shorter events, 32.5 us)
Async XLA Ops:
  2.5 12.6 %collective-permute-start.1 = (bf16[64,2688]{1,0:T(8,128)(2,1)}, bf16[64,2688]{1,0:T(8,128)(2,1)S(1)}, u32[]{:S(2)}, u32[]{:S(2)}) collective-permute-start(bf16[64,2688]{1,0:T(8,128)(2,1)} %get-tuple-element.43.refs_1_), channel_id=1, source_target_pairs={{0,56},{1,57},{2,58},{3,59},{4,60},{5,61},{6,62},{7,63},{8,0},{9,1... | collective-permute-start | bytes 1032200 | tf_op jit(solution)/shard_map/ppermute | solution.py:38
  8.1 10.4 %collective-permute-start = (bf16[64,2688]{1,0:T(8,128)(2,1)}, bf16[64,2688]{1,0:T(8,128)(2,1)S(1)}, u32[]{:S(2)}, u32[]{:S(2)}) collective-permute-start(bf16[64,2688]{1,0:T(8,128)(2,1)} %get-tuple-element.43.refs_1_), channel_id=1, source_target_pairs={{0,8},{1,9},{2,10},{3,11},{4,12},{5,13},{6,14},{7,15},{8,16},{9,17... | collective-permute-start | bytes 1032200 | tf_op jit(solution)/shard_map/ppermute | solution.py:38
  15.2 9.1 %collective-permute-start.3 = (bf16[64,2688]{1,0:T(8,128)(2,1)S(1)}, bf16[64,2688]{1,0:T(8,128)(2,1)S(1)}, u32[]{:S(2)}, u32[]{:S(2)}) collective-permute-start(bf16[64,2688]{1,0:T(8,128)(2,1)S(1)} %collective-permute-done.1.refs_3_), channel_id=1, source_target_pairs={{0,56},{1,57},{2,58},{3,59},{4,60},{5,61},{6,62},{7,63},{8,0},{9,1... | collective-permute-start | bytes 1032200 | tf_op jit(solution)/shard_map/ppermute | solution.py:38
  18.5 9.2 %collective-permute-start.2 = (bf16[64,2688]{1,0:T(8,128)(2,1)S(1)}, bf16[64,2688]{1,0:T(8,128)(2,1)S(1)}, u32[]{:S(2)}, u32[]{:S(2)}) collective-permute-start(bf16[64,2688]{1,0:T(8,128)(2,1)S(1)} %collective-permute-done.refs_2_), channel_id=1, source_target_pairs={{0,8},{1,9},{2,10},{3,11},{4,12},{5,13},{6,14},{7,15},{8,16},{9,17... | collective-permute-start | bytes 1032200 | tf_op jit(solution)/shard_map/ppermute | solution.py:38
  24.3 12.2 %collective-permute-start.6 = (bf16[64,2688]{1,0:T(8,128)(2,1)S(1)}, bf16[64,2688]{1,0:T(8,128)(2,1)S(1)}, u32[]{:S(2)}, u32[]{:S(2)}) collective-permute-start(bf16[64,2688]{1,0:T(8,128)(2,1)S(1)} %collective-permute-done.3.refs_5_), channel_id=1, source_target_pairs={{0,56},{1,57},{2,58},{3,59},{4,60},{5,61},{6,62},{7,63},{8,0},{9,1... | collective-permute-start | bytes 1032200 | tf_op jit(solution)/shard_map/ppermute | solution.py:38
  27.7 11.6 %collective-permute-start.5 = (bf16[64,2688]{1,0:T(8,128)(2,1)S(1)}, bf16[64,2688]{1,0:T(8,128)(2,1)S(1)}, u32[]{:S(2)}, u32[]{:S(2)}) collective-permute-start(bf16[64,2688]{1,0:T(8,128)(2,1)S(1)} %collective-permute-done.2.refs_4_), channel_id=1, source_target_pairs={{0,8},{1,9},{2,10},{3,11},{4,12},{5,13},{6,14},{7,15},{8,16},{9,17... | collective-permute-start | bytes 1032200 | tf_op jit(solution)/shard_map/ppermute | solution.py:38
  31.5 17.0 %collective-permute-start.4 = (bf16[80,2560]{1,0:T(8,128)(2,1)}, bf16[80,2560]{1,0:T(8,128)(2,1)S(1)}, u32[]{:S(2)}, u32[]{:S(2)}) collective-permute-start(bf16[80,2560]{1,0:T(8,128)(2,1)} %get-tuple-element.45), channel_id=1, source_target_pairs={{0,2},{1,3},{2,4},{3,5},{4,6},{5,7},{6,0},{7,1},{8,10},{9,11},{10,... | collective-permute-start | bytes 1228808 | tf_op jit(solution)/shard_map/ppermute | solution.py:38
  32.8 18.4 %collective-permute-start.9 = (bf16[80,2560]{1,0:T(8,128)(2,1)}, bf16[80,2560]{1,0:T(8,128)(2,1)S(1)}, u32[]{:S(2)}, u32[]{:S(2)}) collective-permute-start(bf16[80,2560]{1,0:T(8,128)(2,1)} %get-tuple-element.50), channel_id=1, source_target_pairs={{0,4},{1,5},{2,6},{3,7},{4,0},{5,1},{6,2},{7,3},{8,12},{9,13},{10,... | collective-permute-start | bytes 1228808 | tf_op jit(solution)/shard_map/ppermute | solution.py:38
  35.4 18.3 %collective-permute-start.10 = (bf16[80,2560]{1,0:T(8,128)(2,1)}, bf16[80,2560]{1,0:T(8,128)(2,1)S(1)}, u32[]{:S(2)}, u32[]{:S(2)}) collective-permute-start(bf16[80,2560]{1,0:T(8,128)(2,1)} %get-tuple-element.52), channel_id=1, source_target_pairs={{0,6},{1,7},{2,0},{3,1},{4,2},{5,3},{6,4},{7,5},{8,14},{9,15},{10,... | collective-permute-start | bytes 1228808 | tf_op jit(solution)/shard_map/ppermute | solution.py:38
  36.5 5.1 %collective-permute-start.8 = (bf16[32,2688]{1,0:T(8,128)(2,1)S(1)}, bf16[32,2688]{1,0:T(8,128)(2,1)S(1)}, u32[]{:S(2)}, u32[]{:S(2)}) collective-permute-start(bf16[32,2688]{1,0:T(8,128)(2,1)S(1)} %slice.49), channel_id=1, source_target_pairs={{0,56},{1,57},{2,58},{3,59},{4,60},{5,61},{6,62},{7,63},{8,0},{9,1... | collective-permute-start | bytes 516104 | tf_op jit(solution)/shard_map/ppermute | solution.py:38
  39.3 5.8 %collective-permute-start.7 = (bf16[32,2688]{1,0:T(8,128)(2,1)S(1)}, bf16[32,2688]{1,0:T(8,128)(2,1)S(1)}, u32[]{:S(2)}, u32[]{:S(2)}) collective-permute-start(bf16[32,2688]{1,0:T(8,128)(2,1)S(1)} %slice.48), channel_id=1, source_target_pairs={{0,8},{1,9},{2,10},{3,11},{4,12},{5,13},{6,14},{7,15},{8,16},{9,17... | collective-permute-start | bytes 516104 | tf_op jit(solution)/shard_map/ppermute | solution.py:38
  47.3 11.4 %collective-permute-start.12 = (bf16[48,2560]{1,0:T(8,128)(2,1)}, bf16[48,2560]{1,0:T(8,128)(2,1)S(1)}, u32[]{:S(2)}, u32[]{:S(2)}) collective-permute-start(bf16[48,2560]{1,0:T(8,128)(2,1)} %get-tuple-element.55), channel_id=1, source_target_pairs={{0,2},{1,3},{2,4},{3,5},{4,6},{5,7},{6,0},{7,1},{8,10},{9,11},{10,... | collective-permute-start | bytes 737288 | tf_op jit(solution)/shard_map/ppermute | solution.py:38
  47.5 13.9 %collective-permute-start.13 = (bf16[48,2560]{1,0:T(8,128)(2,1)}, bf16[48,2560]{1,0:T(8,128)(2,1)S(1)}, u32[]{:S(2)}, u32[]{:S(2)}) collective-permute-start(bf16[48,2560]{1,0:T(8,128)(2,1)} %get-tuple-element.56), channel_id=1, source_target_pairs={{0,4},{1,5},{2,6},{3,7},{4,0},{5,1},{6,2},{7,3},{8,12},{9,13},{10,... | collective-permute-start | bytes 737288 | tf_op jit(solution)/shard_map/ppermute | solution.py:38
  48.5 13.6 %collective-permute-start.14 = (bf16[48,2560]{1,0:T(8,128)(2,1)}, bf16[48,2560]{1,0:T(8,128)(2,1)S(1)}, u32[]{:S(2)}, u32[]{:S(2)}) collective-permute-start(bf16[48,2560]{1,0:T(8,128)(2,1)} %get-tuple-element.57), channel_id=1, source_target_pairs={{0,6},{1,7},{2,0},{3,1},{4,2},{5,3},{6,4},{7,5},{8,14},{9,15},{10,... | collective-permute-start | bytes 737288 | tf_op jit(solution)/shard_map/ppermute | solution.py:38
  53.9 13.3 %collective-permute-start.11 = (bf16[160,2560]{1,0:T(8,128)(2,1)S(1)}, bf16[160,2560]{1,0:T(8,128)(2,1)S(1)}, u32[]{:S(2)}, u32[]{:S(2)}) collective-permute-start(bf16[160,2560]{1,0:T(8,128)(2,1)S(1)} %pad_maximum_fusion), channel_id=1, source_target_pairs={{0,1},{1,0},{2,3},{3,2},{4,5},{5,4},{6,7},{7,6},{8,9},{9,8},{10,11... | collective-permute-start | bytes 2457608 | tf_op jit(solution)/shard_map/ppermute | solution.py:38
  62.2 5.0 %collective-permute-start.15 = (bf16[96,2560]{1,0:T(8,128)(2,1)S(1)}, bf16[96,2560]{1,0:T(8,128)(2,1)S(1)}, u32[]{:S(2)}, u32[]{:S(2)}) collective-permute-start(bf16[96,2560]{1,0:T(8,128)(2,1)S(1)} %pad_maximum_fusion.2), channel_id=1, source_target_pairs={{0,1},{1,0},{2,3},{3,2},{4,5},{5,4},{6,7},{7,6},{8,9},{9,8},{10,11... | collective-permute-start | bytes 1474568 | tf_op jit(solution)/shard_map/ppermute | solution.py:38
  148.7 11.0 %collective-permute-start.16 = (bf16[64,2560]{1,0:T(8,128)(2,1)}, bf16[64,2560]{1,0:T(8,128)(2,1)S(1)}, u32[]{:S(2)}, u32[]{:S(2)}) collective-permute-start(bf16[64,2560]{1,0:T(8,128)(2,1)} %bitcast.28), channel_id=1, source_target_pairs={{0,64},{64,128},{128,192},{1,65},{65,129},{129,193},{2,66},{66,130... | collective-permute-start | bytes 983048 | tf_op jit(solution)/shard_map/ppermute | solution.py:303
  162.2 9.1 %collective-permute-start.18 = (bf16[64,2688]{1,0:T(8,128)(2,1)}, bf16[64,2688]{1,0:T(8,128)(2,1)S(1)}, u32[]{:S(2)}, u32[]{:S(2)}) collective-permute-start(bf16[64,2688]{1,0:T(8,128)(2,1)} %get-tuple-element.61.refs_1_), channel_id=1, source_target_pairs={{0,56},{1,57},{2,58},{3,59},{4,60},{5,61},{6,62},{7,63},{8,0},{9,1... | collective-permute-start | bytes 1032200 | tf_op jit(solution)/shard_map/ppermute | solution.py:38
  164.4 10.3 %collective-permute-start.17 = (bf16[64,2688]{1,0:T(8,128)(2,1)}, bf16[64,2688]{1,0:T(8,128)(2,1)S(1)}, u32[]{:S(2)}, u32[]{:S(2)}) collective-permute-start(bf16[64,2688]{1,0:T(8,128)(2,1)} %get-tuple-element.61.refs_1_), channel_id=1, source_target_pairs={{0,8},{1,9},{2,10},{3,11},{4,12},{5,13},{6,14},{7,15},{8,16},{9,17... | collective-permute-start | bytes 1032200 | tf_op jit(solution)/shard_map/ppermute | solution.py:38
  171.4 9.0 %collective-permute-start.20 = (bf16[64,2688]{1,0:T(8,128)(2,1)S(1)}, bf16[64,2688]{1,0:T(8,128)(2,1)S(1)}, u32[]{:S(2)}, u32[]{:S(2)}) collective-permute-start(bf16[64,2688]{1,0:T(8,128)(2,1)S(1)} %collective-permute-done.18.refs_3_), channel_id=1, source_target_pairs={{0,56},{1,57},{2,58},{3,59},{4,60},{5,61},{6,62},{7,63},{8,0},{9,1... | collective-permute-start | bytes 1032200 | tf_op jit(solution)/shard_map/ppermute | solution.py:38
  174.7 9.1 %collective-permute-start.19 = (bf16[64,2688]{1,0:T(8,128)(2,1)S(1)}, bf16[64,2688]{1,0:T(8,128)(2,1)S(1)}, u32[]{:S(2)}, u32[]{:S(2)}) collective-permute-start(bf16[64,2688]{1,0:T(8,128)(2,1)S(1)} %collective-permute-done.17.refs_2_), channel_id=1, source_target_pairs={{0,8},{1,9},{2,10},{3,11},{4,12},{5,13},{6,14},{7,15},{8,16},{9,17... | collective-permute-start | bytes 1032200 | tf_op jit(solution)/shard_map/ppermute | solution.py:38
  180.4 9.3 %collective-permute-start.23 = (bf16[64,2688]{1,0:T(8,128)(2,1)S(1)}, bf16[64,2688]{1,0:T(8,128)(2,1)S(1)}, u32[]{:S(2)}, u32[]{:S(2)}) collective-permute-start(bf16[64,2688]{1,0:T(8,128)(2,1)S(1)} %collective-permute-done.20.refs_5_), channel_id=1, source_target_pairs={{0,56},{1,57},{2,58},{3,59},{4,60},{5,61},{6,62},{7,63},{8,0},{9,1... | collective-permute-start | bytes 1032200 | tf_op jit(solution)/shard_map/ppermute | solution.py:38
  183.8 8.7 %collective-permute-start.22 = (bf16[64,2688]{1,0:T(8,128)(2,1)S(1)}, bf16[64,2688]{1,0:T(8,128)(2,1)S(1)}, u32[]{:S(2)}, u32[]{:S(2)}) collective-permute-start(bf16[64,2688]{1,0:T(8,128)(2,1)S(1)} %collective-permute-done.19.refs_4_), channel_id=1, source_target_pairs={{0,8},{1,9},{2,10},{3,11},{4,12},{5,13},{6,14},{7,15},{8,16},{9,17... | collective-permute-start | bytes 1032200 | tf_op jit(solution)/shard_map/ppermute | solution.py:38
  187.0 15.6 %collective-permute-start.21 = (bf16[80,2560]{1,0:T(8,128)(2,1)}, bf16[80,2560]{1,0:T(8,128)(2,1)S(1)}, u32[]{:S(2)}, u32[]{:S(2)}) collective-permute-start(bf16[80,2560]{1,0:T(8,128)(2,1)} %get-tuple-element.63), channel_id=1, source_target_pairs={{0,2},{1,3},{2,4},{3,5},{4,6},{5,7},{6,0},{7,1},{8,10},{9,11},{10,... | collective-permute-start | bytes 1228808 | tf_op jit(solution)/shard_map/ppermute | solution.py:38
  187.0 17.6 %collective-permute-start.26 = (bf16[80,2560]{1,0:T(8,128)(2,1)}, bf16[80,2560]{1,0:T(8,128)(2,1)S(1)}, u32[]{:S(2)}, u32[]{:S(2)}) collective-permute-start(bf16[80,2560]{1,0:T(8,128)(2,1)} %get-tuple-element.68), channel_id=1, source_target_pairs={{0,4},{1,5},{2,6},{3,7},{4,0},{5,1},{6,2},{7,3},{8,12},{9,13},{10,... | collective-permute-start | bytes 1228808 | tf_op jit(solution)/shard_map/ppermute | solution.py:38
  187.3 22.7 %collective-permute-start.27 = (bf16[80,2560]{1,0:T(8,128)(2,1)}, bf16[80,2560]{1,0:T(8,128)(2,1)S(1)}, u32[]{:S(2)}, u32[]{:S(2)}) collective-permute-start(bf16[80,2560]{1,0:T(8,128)(2,1)} %get-tuple-element.70), channel_id=1, source_target_pairs={{0,6},{1,7},{2,0},{3,1},{4,2},{5,3},{6,4},{7,5},{8,14},{9,15},{10,... | collective-permute-start | bytes 1228808 | tf_op jit(solution)/shard_map/ppermute | solution.py:38
  189.7 5.1 %collective-permute-start.25 = (bf16[32,2688]{1,0:T(8,128)(2,1)S(1)}, bf16[32,2688]{1,0:T(8,128)(2,1)S(1)}, u32[]{:S(2)}, u32[]{:S(2)}) collective-permute-start(bf16[32,2688]{1,0:T(8,128)(2,1)S(1)} %slice.57), channel_id=1, source_target_pairs={{0,56},{1,57},{2,58},{3,59},{4,60},{5,61},{6,62},{7,63},{8,0},{9,1... | collective-permute-start | bytes 516104 | tf_op jit(solution)/shard_map/ppermute | solution.py:38
  192.5 5.8 %collective-permute-start.24 = (bf16[32,2688]{1,0:T(8,128)(2,1)S(1)}, bf16[32,2688]{1,0:T(8,128)(2,1)S(1)}, u32[]{:S(2)}, u32[]{:S(2)}) collective-permute-start(bf16[32,2688]{1,0:T(8,128)(2,1)S(1)} %slice.56), channel_id=1, source_target_pairs={{0,8},{1,9},{2,10},{3,11},{4,12},{5,13},{6,14},{7,15},{8,16},{9,17... | collective-permute-start | bytes 516104 | tf_op jit(solution)/shard_map/ppermute | solution.py:38
  200.5 16.7 %collective-permute-start.29 = (bf16[48,2560]{1,0:T(8,128)(2,1)}, bf16[48,2560]{1,0:T(8,128)(2,1)S(1)}, u32[]{:S(2)}, u32[]{:S(2)}) collective-permute-start(bf16[48,2560]{1,0:T(8,128)(2,1)} %get-tuple-element.73), channel_id=1, source_target_pairs={{0,2},{1,3},{2,4},{3,5},{4,6},{5,7},{6,0},{7,1},{8,10},{9,11},{10,... | collective-permute-start | bytes 737288 | tf_op jit(solution)/shard_map/ppermute | solution.py:38
  200.9 16.3 %collective-permute-start.30 = (bf16[48,2560]{1,0:T(8,128)(2,1)}, bf16[48,2560]{1,0:T(8,128)(2,1)S(1)}, u32[]{:S(2)}, u32[]{:S(2)}) collective-permute-start(bf16[48,2560]{1,0:T(8,128)(2,1)} %get-tuple-element.74), channel_id=1, source_target_pairs={{0,4},{1,5},{2,6},{3,7},{4,0},{5,1},{6,2},{7,3},{8,12},{9,13},{10,... | collective-permute-start | bytes 737288 | tf_op jit(solution)/shard_map/ppermute | solution.py:38
  202.6 14.6 %collective-permute-start.31 = (bf16[48,2560]{1,0:T(8,128)(2,1)}, bf16[48,2560]{1,0:T(8,128)(2,1)S(1)}, u32[]{:S(2)}, u32[]{:S(2)}) collective-permute-start(bf16[48,2560]{1,0:T(8,128)(2,1)} %get-tuple-element.75), channel_id=1, source_target_pairs={{0,6},{1,7},{2,0},{3,1},{4,2},{5,3},{6,4},{7,5},{8,14},{9,15},{10,... | collective-permute-start | bytes 737288 | tf_op jit(solution)/shard_map/ppermute | solution.py:38
  210.1 11.8 %collective-permute-start.28 = (bf16[160,2560]{1,0:T(8,128)(2,1)S(1)}, bf16[160,2560]{1,0:T(8,128)(2,1)S(1)}, u32[]{:S(2)}, u32[]{:S(2)}) collective-permute-start(bf16[160,2560]{1,0:T(8,128)(2,1)S(1)} %pad_maximum_fusion.1), channel_id=1, source_target_pairs={{0,1},{1,0},{2,3},{3,2},{4,5},{5,4},{6,7},{7,6},{8,9},{9,8},{10,11... | collective-permute-start | bytes 2457608 | tf_op jit(solution)/shard_map/ppermute | solution.py:38
  (12 other events, 161.1 us)

commit v2 on v1

--- a/solution.py
+++ b/solution.py
@@ -262,8 +262,8 @@
     tokens = packed.shape[0]
     part = tokens // 2
     below, above = [packed], [packed]
-    for _ in range(2):
-        below.append(along_z(below[-1], 1))
+    for hop in range(2):
+        below.append(along_z(after(below[-1], ids, places) if hop else below[-1], 1))
         above.append(along_z(above[-1], -1))
     near = [packed] + [held_close(value) for value in (below[1], above[1], below[2], above[2])]
     near_rows = dispatch(ids, near, tokens)

time: 304 us -> 304 us (level)
  transfers between devices with their start and end apart: 33 -> 33, of which waited for: 17 -> 18; matrix products, arithmetic and copies ran while one was open for 0% -> 1% of each run, Pallas kernels for 4% -> 4%
where the time goes in v2:
time: 304 us
  blocking collectives  139 us (46%)
  waiting for transfers between devices  64.4 us (21%)
  starting transfers between devices  57.9 us (19%)
  Pallas kernels  40 us (13%)
    all_to_all x2, blocking collectives, section(): lax.all_to_all(outputs, GROUP, split_axis=0, concat_axis=0, tiled=True)  139 us
    ppermute x32, starting transfers between devices, move(): return lax.ppermute(value, GROUP, pairs)  56.6 us
    ppermute x32, waiting for transfers between devices, move(): return lax.ppermute(value, GROUP, pairs)  54.6 us
    pallas_call x2, Pallas kernels, run_experts(): pl.pallas_call(lambda *refs: experts_kernel(len(groups), *refs), out_shap...  19.4 us
    pallas_call x4, Pallas kernels, dispatch(): pl.pallas_call(lambda *refs: dispatch_kernel(block, len(packed), *refs),...  10.8 us
    ppermute x1, waiting for transfers between devices, shards(): lax.ppermute(results[-1][0], 'segment', [(i, i + 1) for i in range(count...  9.76 us
  transfers between devices with their start and end apart: 33, of which 18 were waited for; matrix products, arithmetic and copies ran while one was open for 1% of the time, Pallas kernels for 4%

profile of v2, /device:TPU:7, one launch (start us, length us, event | category | flops | bytes accessed | tf_op | source)
XLA Modules:
  0.0 303.5 jit_solution(290984478241918027)
XLA Ops:
  0.0 2.5 prepare.2
  2.5 5.6 %collective-permute-start.1 = (bf16[64,2688]{1,0:T(8,128)(2,1)}, bf16[64,2688]{1,0:T(8,128)(2,1)S(1)}, u32[]{:S(2)}, u32[]{:S(2)}) collective-permute-start(bf16[64,2688]{1,0:T(8,128)(2,1)} %get-tuple-element.45.refs_1_), channel_id=1, source_target_pairs={{0,56},{1,57},{2,58},{3,59},{4,60},{5,61},{6,62},{7,63},{8,0},{9,1... | collective-permute-start | bytes 1032200 | tf_op jit(solution)/shard_map/ppermute | solution.py:38
  8.8 6.3 %collective-permute-done.1.refs_3_ = bf16[64,2688]{1,0:T(8,128)(2,1)S(1)} collective-permute-done((bf16[64,2688]{1,0:T(8,128)(2,1)}, bf16[64,2688]{1,0:T(8,128)(2,1)S(1)}, u32[]{:S(2)}, u32[]{:S(2)}) %collective-permute-start.1) | collective-permute-done | bytes 344096 | tf_op jit(solution)/shard_map/ppermute | solution.py:38
  15.2 3.3 %collective-permute-start.3 = (bf16[64,2688]{1,0:T(8,128)(2,1)S(1)}, bf16[64,2688]{1,0:T(8,128)(2,1)S(1)}, u32[]{:S(2)}, u32[]{:S(2)}) collective-permute-start(bf16[64,2688]{1,0:T(8,128)(2,1)S(1)} %collective-permute-done.1.refs_3_), channel_id=1, source_target_pairs={{0,56},{1,57},{2,58},{3,59},{4,60},{5,61},{6,62},{7,63},{8,0},{9,1... | collective-permute-start | bytes 1032200 | tf_op jit(solution)/shard_map/ppermute | solution.py:38
  19.0 5.3 %collective-permute-done.3.refs_5_ = bf16[64,2688]{1,0:T(8,128)(2,1)S(1)} collective-permute-done((bf16[64,2688]{1,0:T(8,128)(2,1)S(1)}, bf16[64,2688]{1,0:T(8,128)(2,1)S(1)}, u32[]{:S(2)}, u32[]{:S(2)}) %collective-permute-start.3) | collective-permute-done | bytes 344096 | tf_op jit(solution)/shard_map/ppermute | solution.py:38
  24.3 3.4 %collective-permute-start.6 = (bf16[64,2688]{1,0:T(8,128)(2,1)S(1)}, bf16[64,2688]{1,0:T(8,128)(2,1)S(1)}, u32[]{:S(2)}, u32[]{:S(2)}) collective-permute-start(bf16[64,2688]{1,0:T(8,128)(2,1)S(1)} %collective-permute-done.3.refs_5_), channel_id=1, source_target_pairs={{0,56},{1,57},{2,58},{3,59},{4,60},{5,61},{6,62},{7,63},{8,0},{9,1... | collective-permute-start | bytes 1032200 | tf_op jit(solution)/shard_map/ppermute | solution.py:38
  27.9 3.2 %dispatch.4 = (bf16[40,2560]{1,0:T(8,128)(2,1)}, bf16[40,2560]{1,0:T(8,128)(2,1)}, bf16[80,2560]{1,0:T(8,128)(2,1)}, bf16[80,2560]{1,0:T(8,128)(2,1)}, bf16[80,2560]{1,0:T(8,128)(2,1)}) custom-call(s32[8]{0:T(128)} %fusion.3.refs_0_, bf16[64,2688]{1,0:T(8,128)(2,1)} %get-tuple-element.45.refs_1_, bf16[64,2688]{1,0:T(8,128)(2,1)S(1)} %collective-permute-done.refs_2_, ...), custom_call_target="tpu_custom_call" | custom-call | flops 1000 | bytes 1000 | tf_op jit(solution)/shard_map/dispatch/pallas_call | solution.py:143
  32.4 2.6 collective-permute-start.9
  36.2 2.7 collective-permute-start.8
  41.3 3.5 %collective-permute-done.7.refs_3_ = bf16[32,2688]{1,0:T(8,128)(2,1)S(1)} collective-permute-done((bf16[32,2688]{1,0:T(8,128)(2,1)S(1)}, bf16[32,2688]{1,0:T(8,128)(2,1)S(1)}, u32[]{:S(2)}, u32[]{:S(2)}) %collective-permute-start.7) | collective-permute-done | bytes 172064 | tf_op jit(solution)/shard_map/ppermute | solution.py:38
  50.8 2.5 collective-permute-done.10.refs_4_
  53.5 4.8 %collective-permute-start.11 = (bf16[160,2560]{1,0:T(8,128)(2,1)S(1)}, bf16[160,2560]{1,0:T(8,128)(2,1)S(1)}, u32[]{:S(2)}, u32[]{:S(2)}) collective-permute-start(bf16[160,2560]{1,0:T(8,128)(2,1)S(1)} %pad_maximum_fusion), channel_id=1, source_target_pairs={{0,1},{1,0},{2,3},{3,2},{4,5},{5,4},{6,7},{7,6},{8,9},{9,8},{10,11... | collective-permute-start | bytes 2457608 | tf_op jit(solution)/shard_map/ppermute | solution.py:38
  58.3 2.8 collective-permute-done.13.refs_8_
  61.8 3.5 %collective-permute-start.15 = (bf16[96,2560]{1,0:T(8,128)(2,1)S(1)}, bf16[96,2560]{1,0:T(8,128)(2,1)S(1)}, u32[]{:S(2)}, u32[]{:S(2)}) collective-permute-start(bf16[96,2560]{1,0:T(8,128)(2,1)S(1)} %pad_maximum_fusion.2), channel_id=1, source_target_pairs={{0,1},{1,0},{2,3},{3,2},{4,5},{5,4},{6,7},{7,6},{8,9},{9,8},{10,11... | collective-permute-start | bytes 1474568 | tf_op jit(solution)/shard_map/ppermute | solution.py:38
  66.9 9.7 %experts.2 = bf16[64,8,2560]{2,1,0:T(8,128)(2,1)S(1)} custom-call(s32[64]{0:T(128)S(1)} %fusion.1.refs_0_, bf16[40,2560]{1,0:T(8,128)(2,1)S(1)} %copy-done.1, bf16[80,2560]{1,0:T(8,128)(2,1)S(1)} %collective-permute-done.4.refs_2_, bf16[80,2560]{1,0:T(8,128)(2,1)S(1)} %collective-permute-done.9.refs_3_, ...), custom_call_target="tpu_custom_call" | custom-call | flops 1000 | bytes 1000 | tf_op jit(solution)/shard_map/experts/pallas_call | solution.py:217
  76.6 69.5 %all_to_all.10 = bf16[64,8,2560]{2,1,0:T(8,128)(2,1)S(1)} all-to-all(bf16[64,8,2560]{2,1,0:T(8,128)(2,1)S(1)} %experts.2), channel_id=1, replica_groups=mesh['segment'=4,'expert'=32,'dp'=2] {'expert','dp'}, dimensions={0} | all-to-all | bytes 5242880 | tf_op jit(solution)/shard_map/all_to_all | solution.py:278
  149.7 9.8 %collective-permute-done.16.refs_1_ = bf16[64,2560]{1,0:T(8,128)(2,1)S(1)} collective-permute-done((bf16[64,2560]{1,0:T(8,128)(2,1)}, bf16[64,2560]{1,0:T(8,128)(2,1)S(1)}, u32[]{:S(2)}, u32[]{:S(2)}) %collective-permute-start.16) | collective-permute-done | bytes 327712 | tf_op jit(solution)/shard_map/ppermute | solution.py:303
  159.4 2.5 prepare.3
  164.0 7.0 %collective-permute-done.18.refs_3_ = bf16[64,2688]{1,0:T(8,128)(2,1)S(1)} collective-permute-done((bf16[64,2688]{1,0:T(8,128)(2,1)}, bf16[64,2688]{1,0:T(8,128)(2,1)S(1)}, u32[]{:S(2)}, u32[]{:S(2)}) %collective-permute-start.18) | collective-permute-done | bytes 344096 | tf_op jit(solution)/shard_map/ppermute | solution.py:38
  171.0 3.3 %collective-permute-start.20 = (bf16[64,2688]{1,0:T(8,128)(2,1)S(1)}, bf16[64,2688]{1,0:T(8,128)(2,1)S(1)}, u32[]{:S(2)}, u32[]{:S(2)}) collective-permute-start(bf16[64,2688]{1,0:T(8,128)(2,1)S(1)} %collective-permute-done.18.refs_3_), channel_id=1, source_target_pairs={{0,56},{1,57},{2,58},{3,59},{4,60},{5,61},{6,62},{7,63},{8,0},{9,1... | collective-permute-start | bytes 1032200 | tf_op jit(solution)/shard_map/ppermute | solution.py:38
  174.3 5.7 %collective-permute-done.20.refs_5_ = bf16[64,2688]{1,0:T(8,128)(2,1)S(1)} collective-permute-done((bf16[64,2688]{1,0:T(8,128)(2,1)S(1)}, bf16[64,2688]{1,0:T(8,128)(2,1)S(1)}, u32[]{:S(2)}, u32[]{:S(2)}) %collective-permute-start.20) | collective-permute-done | bytes 344096 | tf_op jit(solution)/shard_map/ppermute | solution.py:38
  180.0 3.4 %collective-permute-start.23 = (bf16[64,2688]{1,0:T(8,128)(2,1)S(1)}, bf16[64,2688]{1,0:T(8,128)(2,1)S(1)}, u32[]{:S(2)}, u32[]{:S(2)}) collective-permute-start(bf16[64,2688]{1,0:T(8,128)(2,1)S(1)} %collective-permute-done.20.refs_5_), channel_id=1, source_target_pairs={{0,56},{1,57},{2,58},{3,59},{4,60},{5,61},{6,62},{7,63},{8,0},{9,1... | collective-permute-start | bytes 1032200 | tf_op jit(solution)/shard_map/ppermute | solution.py:38
  183.5 3.2 %dispatch.6 = (bf16[40,2560]{1,0:T(8,128)(2,1)}, bf16[40,2560]{1,0:T(8,128)(2,1)}, bf16[80,2560]{1,0:T(8,128)(2,1)}, bf16[80,2560]{1,0:T(8,128)(2,1)}, bf16[80,2560]{1,0:T(8,128)(2,1)}) custom-call(s32[8]{0:T(128)} %fusion.3.refs_0_, bf16[64,2688]{1,0:T(8,128)(2,1)} %get-tuple-element.64.refs_1_, bf16[64,2688]{1,0:T(8,128)(2,1)S(1)} %collective-permute-done.17.refs_2_, ...), custom_call_target="tpu_custom_call" | custom-call | flops 1000 | bytes 1000 | tf_op jit(solution)/shard_map/dispatch/pallas_call | solution.py:143
  189.4 2.8 collective-permute-start.25
  194.5 3.5 %collective-permute-done.24.refs_3_ = bf16[32,2688]{1,0:T(8,128)(2,1)S(1)} collective-permute-done((bf16[32,2688]{1,0:T(8,128)(2,1)S(1)}, bf16[32,2688]{1,0:T(8,128)(2,1)S(1)}, u32[]{:S(2)}, u32[]{:S(2)}) %collective-permute-start.24) | collective-permute-done | bytes 172064 | tf_op jit(solution)/shard_map/ppermute | solution.py:38
  204.3 5.2 %collective-permute-done.27.refs_4_ = bf16[80,2560]{1,0:T(8,128)(2,1)S(1)} collective-permute-done((bf16[80,2560]{1,0:T(8,128)(2,1)}, bf16[80,2560]{1,0:T(8,128)(2,1)S(1)}, u32[]{:S(2)}, u32[]{:S(2)}) %collective-permute-start.27) | collective-permute-done | bytes 409632 | tf_op jit(solution)/shard_map/ppermute | solution.py:38
  209.7 3.9 %collective-permute-start.28 = (bf16[160,2560]{1,0:T(8,128)(2,1)S(1)}, bf16[160,2560]{1,0:T(8,128)(2,1)S(1)}, u32[]{:S(2)}, u32[]{:S(2)}) collective-permute-start(bf16[160,2560]{1,0:T(8,128)(2,1)S(1)} %pad_maximum_fusion.1), channel_id=1, source_target_pairs={{0,1},{1,0},{2,3},{3,2},{4,5},{5,4},{6,7},{7,6},{8,9},{9,8},{10,11... | collective-permute-start | bytes 2457608 | tf_op jit(solution)/shard_map/ppermute | solution.py:38
  213.6 3.2 %collective-permute-done.29.refs_7_ = bf16[48,2560]{1,0:T(8,128)(2,1)S(1)} collective-permute-done((bf16[48,2560]{1,0:T(8,128)(2,1)}, bf16[48,2560]{1,0:T(8,128)(2,1)S(1)}, u32[]{:S(2)}, u32[]{:S(2)}) %collective-permute-start.29) | collective-permute-done | bytes 245792 | tf_op jit(solution)/shard_map/ppermute | solution.py:38
  216.9 3.1 %collective-permute-start.32 = (bf16[96,2560]{1,0:T(8,128)(2,1)S(1)}, bf16[96,2560]{1,0:T(8,128)(2,1)S(1)}, u32[]{:S(2)}, u32[]{:S(2)}) collective-permute-start(bf16[96,2560]{1,0:T(8,128)(2,1)S(1)} %pad_maximum_fusion.3), channel_id=1, source_target_pairs={{0,1},{1,0},{2,3},{3,2},{4,5},{5,4},{6,7},{7,6},{8,9},{9,8},{10,11... | collective-permute-start | bytes 1474568 | tf_op jit(solution)/shard_map/ppermute | solution.py:38
  221.6 9.7 %experts.3 = bf16[64,8,2560]{2,1,0:T(8,128)(2,1)S(1)} custom-call(s32[64]{0:T(128)S(1)} %fusion.1.refs_0_, bf16[40,2560]{1,0:T(8,128)(2,1)S(1)} %copy-done, bf16[80,2560]{1,0:T(8,128)(2,1)S(1)} %collective-permute-done.21.refs_2_, bf16[80,2560]{1,0:T(8,128)(2,1)S(1)} %collective-permute-done.26.refs_3_, ...), custom_call_target="tpu_custom_call" | custom-call | flops 1000 | bytes 1000 | tf_op jit(solution)/shard_map/experts/pallas_call | solution.py:217
  231.3 69.8 %all_to_all.11 = bf16[64,8,2560]{2,1,0:T(8,128)(2,1)S(1)} all-to-all(bf16[64,8,2560]{2,1,0:T(8,128)(2,1)S(1)} %experts.3), channel_id=1, replica_groups=mesh['segment'=4,'expert'=32,'dp'=2] {'expert','dp'}, dimensions={0} | all-to-all | bytes 5242880 | tf_op jit(solution)/shard_map/all_to_all | solution.py:278
  301.0 2.5 combine.3
  (84 shorter events, 33.3 us)
Async XLA Ops:
  2.5 12.6 %collective-permute-start.1 = (bf16[64,2688]{1,0:T(8,128)(2,1)}, bf16[64,2688]{1,0:T(8,128)(2,1)S(1)}, u32[]{:S(2)}, u32[]{:S(2)}) collective-permute-start(bf16[64,2688]{1,0:T(8,128)(2,1)} %get-tuple-element.45.refs_1_), channel_id=1, source_target_pairs={{0,56},{1,57},{2,58},{3,59},{4,60},{5,61},{6,62},{7,63},{8,0},{9,1... | collective-permute-start | bytes 1032200 | tf_op jit(solution)/shard_map/ppermute | solution.py:38
  8.1 10.8 %collective-permute-start = (bf16[64,2688]{1,0:T(8,128)(2,1)}, bf16[64,2688]{1,0:T(8,128)(2,1)S(1)}, u32[]{:S(2)}, u32[]{:S(2)}) collective-permute-start(bf16[64,2688]{1,0:T(8,128)(2,1)} %get-tuple-element.45.refs_1_), channel_id=1, source_target_pairs={{0,8},{1,9},{2,10},{3,11},{4,12},{5,13},{6,14},{7,15},{8,16},{9,17... | collective-permute-start | bytes 1032200 | tf_op jit(solution)/shard_map/ppermute | solution.py:38
  15.2 9.1 %collective-permute-start.3 = (bf16[64,2688]{1,0:T(8,128)(2,1)S(1)}, bf16[64,2688]{1,0:T(8,128)(2,1)S(1)}, u32[]{:S(2)}, u32[]{:S(2)}) collective-permute-start(bf16[64,2688]{1,0:T(8,128)(2,1)S(1)} %collective-permute-done.1.refs_3_), channel_id=1, source_target_pairs={{0,56},{1,57},{2,58},{3,59},{4,60},{5,61},{6,62},{7,63},{8,0},{9,1... | collective-permute-start | bytes 1032200 | tf_op jit(solution)/shard_map/ppermute | solution.py:38
  19.0 8.9 %collective-permute-start.2 = (bf16[64,2688]{1,0:T(8,128)(2,1)S(1)}, bf16[64,2688]{1,0:T(8,128)(2,1)S(1)}, u32[]{:S(2)}, u32[]{:S(2)}) collective-permute-start(bf16[64,2688]{1,0:T(8,128)(2,1)S(1)} %collective-permute-done.refs_2_), channel_id=1, source_target_pairs={{0,8},{1,9},{2,10},{3,11},{4,12},{5,13},{6,14},{7,15},{8,16},{9,17... | collective-permute-start | bytes 1032200 | tf_op jit(solution)/shard_map/ppermute | solution.py:38
  24.3 11.8 %collective-permute-start.6 = (bf16[64,2688]{1,0:T(8,128)(2,1)S(1)}, bf16[64,2688]{1,0:T(8,128)(2,1)S(1)}, u32[]{:S(2)}, u32[]{:S(2)}) collective-permute-start(bf16[64,2688]{1,0:T(8,128)(2,1)S(1)} %collective-permute-done.3.refs_5_), channel_id=1, source_target_pairs={{0,56},{1,57},{2,58},{3,59},{4,60},{5,61},{6,62},{7,63},{8,0},{9,1... | collective-permute-start | bytes 1032200 | tf_op jit(solution)/shard_map/ppermute | solution.py:38
  27.9 11.0 %collective-permute-start.5 = (bf16[64,2688]{1,0:T(8,128)(2,1)S(1)}, bf16[64,2688]{1,0:T(8,128)(2,1)S(1)}, u32[]{:S(2)}, u32[]{:S(2)}) collective-permute-start(bf16[64,2688]{1,0:T(8,128)(2,1)S(1)} %collective-permute-done.2.refs_4_), channel_id=1, source_target_pairs={{0,8},{1,9},{2,10},{3,11},{4,12},{5,13},{6,14},{7,15},{8,16},{9,17... | collective-permute-start | bytes 1032200 | tf_op jit(solution)/shard_map/ppermute | solution.py:38
  31.1 17.0 %collective-permute-start.4 = (bf16[80,2560]{1,0:T(8,128)(2,1)}, bf16[80,2560]{1,0:T(8,128)(2,1)S(1)}, u32[]{:S(2)}, u32[]{:S(2)}) collective-permute-start(bf16[80,2560]{1,0:T(8,128)(2,1)} %get-tuple-element.48), channel_id=1, source_target_pairs={{0,2},{1,3},{2,4},{3,5},{4,6},{5,7},{6,0},{7,1},{8,10},{9,11},{10,... | collective-permute-start | bytes 1228808 | tf_op jit(solution)/shard_map/ppermute | solution.py:38
  32.4 18.4 %collective-permute-start.9 = (bf16[80,2560]{1,0:T(8,128)(2,1)}, bf16[80,2560]{1,0:T(8,128)(2,1)S(1)}, u32[]{:S(2)}, u32[]{:S(2)}) collective-permute-start(bf16[80,2560]{1,0:T(8,128)(2,1)} %get-tuple-element.53), channel_id=1, source_target_pairs={{0,4},{1,5},{2,6},{3,7},{4,0},{5,1},{6,2},{7,3},{8,12},{9,13},{10,... | collective-permute-start | bytes 1228808 | tf_op jit(solution)/shard_map/ppermute | solution.py:38
  35.1 18.3 %collective-permute-start.10 = (bf16[80,2560]{1,0:T(8,128)(2,1)}, bf16[80,2560]{1,0:T(8,128)(2,1)S(1)}, u32[]{:S(2)}, u32[]{:S(2)}) collective-permute-start(bf16[80,2560]{1,0:T(8,128)(2,1)} %get-tuple-element.55), channel_id=1, source_target_pairs={{0,6},{1,7},{2,0},{3,1},{4,2},{5,3},{6,4},{7,5},{8,14},{9,15},{10,... | collective-permute-start | bytes 1228808 | tf_op jit(solution)/shard_map/ppermute | solution.py:38
  36.2 5.1 %collective-permute-start.8 = (bf16[32,2688]{1,0:T(8,128)(2,1)S(1)}, bf16[32,2688]{1,0:T(8,128)(2,1)S(1)}, u32[]{:S(2)}, u32[]{:S(2)}) collective-permute-start(bf16[32,2688]{1,0:T(8,128)(2,1)S(1)} %slice.49), channel_id=1, source_target_pairs={{0,56},{1,57},{2,58},{3,59},{4,60},{5,61},{6,62},{7,63},{8,0},{9,1... | collective-permute-start | bytes 516104 | tf_op jit(solution)/shard_map/ppermute | solution.py:38
  38.9 5.8 %collective-permute-start.7 = (bf16[32,2688]{1,0:T(8,128)(2,1)S(1)}, bf16[32,2688]{1,0:T(8,128)(2,1)S(1)}, u32[]{:S(2)}, u32[]{:S(2)}) collective-permute-start(bf16[32,2688]{1,0:T(8,128)(2,1)S(1)} %slice.48), channel_id=1, source_target_pairs={{0,8},{1,9},{2,10},{3,11},{4,12},{5,13},{6,14},{7,15},{8,16},{9,17... | collective-permute-start | bytes 516104 | tf_op jit(solution)/shard_map/ppermute | solution.py:38
  46.9 11.3 %collective-permute-start.12 = (bf16[48,2560]{1,0:T(8,128)(2,1)}, bf16[48,2560]{1,0:T(8,128)(2,1)S(1)}, u32[]{:S(2)}, u32[]{:S(2)}) collective-permute-start(bf16[48,2560]{1,0:T(8,128)(2,1)} %get-tuple-element.58), channel_id=1, source_target_pairs={{0,2},{1,3},{2,4},{3,5},{4,6},{5,7},{6,0},{7,1},{8,10},{9,11},{10,... | collective-permute-start | bytes 737288 | tf_op jit(solution)/shard_map/ppermute | solution.py:38
  47.2 13.9 %collective-permute-start.13 = (bf16[48,2560]{1,0:T(8,128)(2,1)}, bf16[48,2560]{1,0:T(8,128)(2,1)S(1)}, u32[]{:S(2)}, u32[]{:S(2)}) collective-permute-start(bf16[48,2560]{1,0:T(8,128)(2,1)} %get-tuple-element.59), channel_id=1, source_target_pairs={{0,4},{1,5},{2,6},{3,7},{4,0},{5,1},{6,2},{7,3},{8,12},{9,13},{10,... | collective-permute-start | bytes 737288 | tf_op jit(solution)/shard_map/ppermute | solution.py:38
  48.1 13.6 %collective-permute-start.14 = (bf16[48,2560]{1,0:T(8,128)(2,1)}, bf16[48,2560]{1,0:T(8,128)(2,1)S(1)}, u32[]{:S(2)}, u32[]{:S(2)}) collective-permute-start(bf16[48,2560]{1,0:T(8,128)(2,1)} %get-tuple-element.60), channel_id=1, source_target_pairs={{0,6},{1,7},{2,0},{3,1},{4,2},{5,3},{6,4},{7,5},{8,14},{9,15},{10,... | collective-permute-start | bytes 737288 | tf_op jit(solution)/shard_map/ppermute | solution.py:38
  53.5 13.4 %collective-permute-start.11 = (bf16[160,2560]{1,0:T(8,128)(2,1)S(1)}, bf16[160,2560]{1,0:T(8,128)(2,1)S(1)}, u32[]{:S(2)}, u32[]{:S(2)}) collective-permute-start(bf16[160,2560]{1,0:T(8,128)(2,1)S(1)} %pad_maximum_fusion), channel_id=1, source_target_pairs={{0,1},{1,0},{2,3},{3,2},{4,5},{5,4},{6,7},{7,6},{8,9},{9,8},{10,11... | collective-permute-start | bytes 2457608 | tf_op jit(solution)/shard_map/ppermute | solution.py:38
  61.8 5.0 %collective-permute-start.15 = (bf16[96,2560]{1,0:T(8,128)(2,1)S(1)}, bf16[96,2560]{1,0:T(8,128)(2,1)S(1)}, u32[]{:S(2)}, u32[]{:S(2)}) collective-permute-start(bf16[96,2560]{1,0:T(8,128)(2,1)S(1)} %pad_maximum_fusion.2), channel_id=1, source_target_pairs={{0,1},{1,0},{2,3},{3,2},{4,5},{5,4},{6,7},{7,6},{8,9},{9,8},{10,11... | collective-permute-start | bytes 1474568 | tf_op jit(solution)/shard_map/ppermute | solution.py:38
  148.4 11.1 %collective-permute-start.16 = (bf16[64,2560]{1,0:T(8,128)(2,1)}, bf16[64,2560]{1,0:T(8,128)(2,1)S(1)}, u32[]{:S(2)}, u32[]{:S(2)}) collective-permute-start(bf16[64,2560]{1,0:T(8,128)(2,1)} %bitcast.28), channel_id=1, source_target_pairs={{0,64},{64,128},{128,192},{1,65},{65,129},{129,193},{2,66},{66,130... | collective-permute-start | bytes 983048 | tf_op jit(solution)/shard_map/ppermute | solution.py:303
  161.9 9.1 %collective-permute-start.18 = (bf16[64,2688]{1,0:T(8,128)(2,1)}, bf16[64,2688]{1,0:T(8,128)(2,1)S(1)}, u32[]{:S(2)}, u32[]{:S(2)}) collective-permute-start(bf16[64,2688]{1,0:T(8,128)(2,1)} %get-tuple-element.64.refs_1_), channel_id=1, source_target_pairs={{0,56},{1,57},{2,58},{3,59},{4,60},{5,61},{6,62},{7,63},{8,0},{9,1... | collective-permute-start | bytes 1032200 | tf_op jit(solution)/shard_map/ppermute | solution.py:38
  164.0 10.3 %collective-permute-start.17 = (bf16[64,2688]{1,0:T(8,128)(2,1)}, bf16[64,2688]{1,0:T(8,128)(2,1)S(1)}, u32[]{:S(2)}, u32[]{:S(2)}) collective-permute-start(bf16[64,2688]{1,0:T(8,128)(2,1)} %get-tuple-element.64.refs_1_), channel_id=1, source_target_pairs={{0,8},{1,9},{2,10},{3,11},{4,12},{5,13},{6,14},{7,15},{8,16},{9,17... | collective-permute-start | bytes 1032200 | tf_op jit(solution)/shard_map/ppermute | solution.py:38
  171.0 9.0 %collective-permute-start.20 = (bf16[64,2688]{1,0:T(8,128)(2,1)S(1)}, bf16[64,2688]{1,0:T(8,128)(2,1)S(1)}, u32[]{:S(2)}, u32[]{:S(2)}) collective-permute-start(bf16[64,2688]{1,0:T(8,128)(2,1)S(1)} %collective-permute-done.18.refs_3_), channel_id=1, source_target_pairs={{0,56},{1,57},{2,58},{3,59},{4,60},{5,61},{6,62},{7,63},{8,0},{9,1... | collective-permute-start | bytes 1032200 | tf_op jit(solution)/shard_map/ppermute | solution.py:38
  174.3 9.1 %collective-permute-start.19 = (bf16[64,2688]{1,0:T(8,128)(2,1)S(1)}, bf16[64,2688]{1,0:T(8,128)(2,1)S(1)}, u32[]{:S(2)}, u32[]{:S(2)}) collective-permute-start(bf16[64,2688]{1,0:T(8,128)(2,1)S(1)} %collective-permute-done.17.refs_2_), channel_id=1, source_target_pairs={{0,8},{1,9},{2,10},{3,11},{4,12},{5,13},{6,14},{7,15},{8,16},{9,17... | collective-permute-start | bytes 1032200 | tf_op jit(solution)/shard_map/ppermute | solution.py:38
  180.0 9.3 %collective-permute-start.23 = (bf16[64,2688]{1,0:T(8,128)(2,1)S(1)}, bf16[64,2688]{1,0:T(8,128)(2,1)S(1)}, u32[]{:S(2)}, u32[]{:S(2)}) collective-permute-start(bf16[64,2688]{1,0:T(8,128)(2,1)S(1)} %collective-permute-done.20.refs_5_), channel_id=1, source_target_pairs={{0,56},{1,57},{2,58},{3,59},{4,60},{5,61},{6,62},{7,63},{8,0},{9,1... | collective-permute-start | bytes 1032200 | tf_op jit(solution)/shard_map/ppermute | solution.py:38
  183.4 8.7 %collective-permute-start.22 = (bf16[64,2688]{1,0:T(8,128)(2,1)S(1)}, bf16[64,2688]{1,0:T(8,128)(2,1)S(1)}, u32[]{:S(2)}, u32[]{:S(2)}) collective-permute-start(bf16[64,2688]{1,0:T(8,128)(2,1)S(1)} %collective-permute-done.19.refs_4_), channel_id=1, source_target_pairs={{0,8},{1,9},{2,10},{3,11},{4,12},{5,13},{6,14},{7,15},{8,16},{9,17... | collective-permute-start | bytes 1032200 | tf_op jit(solution)/shard_map/ppermute | solution.py:38
  186.7 15.6 %collective-permute-start.21 = (bf16[80,2560]{1,0:T(8,128)(2,1)}, bf16[80,2560]{1,0:T(8,128)(2,1)S(1)}, u32[]{:S(2)}, u32[]{:S(2)}) collective-permute-start(bf16[80,2560]{1,0:T(8,128)(2,1)} %get-tuple-element.67), channel_id=1, source_target_pairs={{0,2},{1,3},{2,4},{3,5},{4,6},{5,7},{6,0},{7,1},{8,10},{9,11},{10,... | collective-permute-start | bytes 1228808 | tf_op jit(solution)/shard_map/ppermute | solution.py:38
  186.7 17.7 %collective-permute-start.26 = (bf16[80,2560]{1,0:T(8,128)(2,1)}, bf16[80,2560]{1,0:T(8,128)(2,1)S(1)}, u32[]{:S(2)}, u32[]{:S(2)}) collective-permute-start(bf16[80,2560]{1,0:T(8,128)(2,1)} %get-tuple-element.72), channel_id=1, source_target_pairs={{0,4},{1,5},{2,6},{3,7},{4,0},{5,1},{6,2},{7,3},{8,12},{9,13},{10,... | collective-permute-start | bytes 1228808 | tf_op jit(solution)/shard_map/ppermute | solution.py:38
  186.9 22.7 %collective-permute-start.27 = (bf16[80,2560]{1,0:T(8,128)(2,1)}, bf16[80,2560]{1,0:T(8,128)(2,1)S(1)}, u32[]{:S(2)}, u32[]{:S(2)}) collective-permute-start(bf16[80,2560]{1,0:T(8,128)(2,1)} %get-tuple-element.74), channel_id=1, source_target_pairs={{0,6},{1,7},{2,0},{3,1},{4,2},{5,3},{6,4},{7,5},{8,14},{9,15},{10,... | collective-permute-start | bytes 1228808 | tf_op jit(solution)/shard_map/ppermute | solution.py:38
  189.4 5.1 %collective-permute-start.25 = (bf16[32,2688]{1,0:T(8,128)(2,1)S(1)}, bf16[32,2688]{1,0:T(8,128)(2,1)S(1)}, u32[]{:S(2)}, u32[]{:S(2)}) collective-permute-start(bf16[32,2688]{1,0:T(8,128)(2,1)S(1)} %slice.57), channel_id=1, source_target_pairs={{0,56},{1,57},{2,58},{3,59},{4,60},{5,61},{6,62},{7,63},{8,0},{9,1... | collective-permute-start | bytes 516104 | tf_op jit(solution)/shard_map/ppermute | solution.py:38
  192.1 5.8 %collective-permute-start.24 = (bf16[32,2688]{1,0:T(8,128)(2,1)S(1)}, bf16[32,2688]{1,0:T(8,128)(2,1)S(1)}, u32[]{:S(2)}, u32[]{:S(2)}) collective-permute-start(bf16[32,2688]{1,0:T(8,128)(2,1)S(1)} %slice.56), channel_id=1, source_target_pairs={{0,8},{1,9},{2,10},{3,11},{4,12},{5,13},{6,14},{7,15},{8,16},{9,17... | collective-permute-start | bytes 516104 | tf_op jit(solution)/shard_map/ppermute | solution.py:38
  200.1 16.7 %collective-permute-start.29 = (bf16[48,2560]{1,0:T(8,128)(2,1)}, bf16[48,2560]{1,0:T(8,128)(2,1)S(1)}, u32[]{:S(2)}, u32[]{:S(2)}) collective-permute-start(bf16[48,2560]{1,0:T(8,128)(2,1)} %get-tuple-element.77), channel_id=1, source_target_pairs={{0,2},{1,3},{2,4},{3,5},{4,6},{5,7},{6,0},{7,1},{8,10},{9,11},{10,... | collective-permute-start | bytes 737288 | tf_op jit(solution)/shard_map/ppermute | solution.py:38
  200.6 16.3 %collective-permute-start.30 = (bf16[48,2560]{1,0:T(8,128)(2,1)}, bf16[48,2560]{1,0:T(8,128)(2,1)S(1)}, u32[]{:S(2)}, u32[]{:S(2)}) collective-permute-start(bf16[48,2560]{1,0:T(8,128)(2,1)} %get-tuple-element.78), channel_id=1, source_target_pairs={{0,4},{1,5},{2,6},{3,7},{4,0},{5,1},{6,2},{7,3},{8,12},{9,13},{10,... | collective-permute-start | bytes 737288 | tf_op jit(solution)/shard_map/ppermute | solution.py:38
  202.2 14.6 %collective-permute-start.31 = (bf16[48,2560]{1,0:T(8,128)(2,1)}, bf16[48,2560]{1,0:T(8,128)(2,1)S(1)}, u32[]{:S(2)}, u32[]{:S(2)}) collective-permute-start(bf16[48,2560]{1,0:T(8,128)(2,1)} %get-tuple-element.79), channel_id=1, source_target_pairs={{0,6},{1,7},{2,0},{3,1},{4,2},{5,3},{6,4},{7,5},{8,14},{9,15},{10,... | collective-permute-start | bytes 737288 | tf_op jit(solution)/shard_map/ppermute | solution.py:38
  209.7 11.8 %collective-permute-start.28 = (bf16[160,2560]{1,0:T(8,128)(2,1)S(1)}, bf16[160,2560]{1,0:T(8,128)(2,1)S(1)}, u32[]{:S(2)}, u32[]{:S(2)}) collective-permute-start(bf16[160,2560]{1,0:T(8,128)(2,1)S(1)} %pad_maximum_fusion.1), channel_id=1, source_target_pairs={{0,1},{1,0},{2,3},{3,2},{4,5},{5,4},{6,7},{7,6},{8,9},{9,8},{10,11... | collective-permute-start | bytes 2457608 | tf_op jit(solution)/shard_map/ppermute | solution.py:38
  (9 other events, 125.3 us)
